TPU v7x, 512 devices: a whole 4x4x16 slice. The times are simulated.
512 devices in a mesh: seq: 64 (over z, y), head: 8 (over x, core).
Axes of the slice: x: 4, y: 4, z: 16, core: 2. Of those that a mesh axis runs over, the one named last changes fastest.
Arguments:
- stream_x: bfloat16 [16384, 3072], P('seq', 'head')
- qkv_weight: bfloat16 [3072, 4608], P(None, 'head')
- short_lengths: int32 [32], replicated, may hold values from 1 to 256, 4096 in all
- cache_owner: int32 [16384, 1], P('seq'), may hold values from 0 to 63, as said below
Outputs:
- attended: bfloat16 [16384, 1536], P('seq', 'head')
- row_lse: float32 [16, 16384], P('head', 'seq')
- kv_cache: bfloat16 [32768, 3072], P('seq', 'head')
Inputs may be any that keep to these rules, and one draw needn't show every extreme that they name: `short_lengths`: the lengths sum to 4096 and the longest is exactly 256. `cache_owner`: the rows of one device form 256 / 8 aligned pages of 8 rows; all rows of a page name the same owner, and the pages of one device name different owners, so an owner takes either none or exactly 8 rows of one device.
All inputs are finite; a program needn't handle non-finite values.
Results may differ from a plain program's by a relative error of at most 0.0083.
Values may be sent and summed in bfloat16 or wider, within the bound.
No kernel may reach another device: no remote copies, remote signals or barrier semaphores. Data moves between devices by JAX's collectives and lax.ppermute only.
A program may use at most 128 MiB of HBM per device.

v0:
```python
import functools
import math

import jax
import jax.numpy as jnp
from jax import lax
from jax.experimental import pallas as pl
from jax.experimental.pallas import tpu as pltpu
from jax.sharding import Mesh, PartitionSpec as P

HD = 96
CAP = 8
neg_large = -1e30
rope_base = 10000.0
score_scale = 1.0 / math.sqrt(HD)
log2_scale = score_scale * math.log2(math.e)


def boundaries(short_lengths, long_length):
    count = short_lengths.shape[0]
    before = jnp.arange(count)[None, :] < jnp.arange(count + 1)[:, None]
    return jnp.sum(jnp.where(before, short_lengths[None, :], 0), axis=1) + long_length


PAIR = 2
KEYS = 256
MESH_Y = 4


def lane_ids(shape):
    return lax.broadcasted_iota(jnp.int32, shape, 1)


def block_sum(core, x_ref, w_ref):
    rows = 256
    depth = x_ref.shape[1]
    total = None
    for i in range(x_ref.shape[0] // rows):
        first = pl.multiple_of((2 * i + core) * depth, 128)
        part = lax.dot_general(
            x_ref[i * rows : (i + 1) * rows, :],
            w_ref[:, pl.ds(first, depth)],
            (((1,), (1,)), ((), ())),
            preferred_element_type=jnp.float32,
        )
        total = part if total is None else total + part
    return total


def half_projection(core_ref, x_ref, w_ref, out_ref):
    out_ref[...] = block_sum(core_ref[0], x_ref, w_ref)


def pack_heads(p0, p1, p2, p3):
    lanes = lane_ids(p0.shape)
    r1 = pltpu.roll(p1, 96, 1)
    r2 = pltpu.roll(p2, 64, 1)
    r3 = pltpu.roll(p3, 32, 1)
    return (
        jnp.where(lanes < 96, p0, r1),
        jnp.where(lanes < 64, r1, r2),
        jnp.where(lanes < 32, r2, r3),
    )


def rest_projection(core_ref, x_ref, w_ref, first_ref, cos_ref, sin_ref, q_ref, kv_ref):
    total = first_ref[...] + block_sum(core_ref[0], x_ref, w_ref)
    rows, columns = total.shape
    width = columns + 64
    whole = jnp.concatenate([total, jnp.zeros((rows, 64), jnp.float32)], axis=1)
    cosine = cos_ref[...]
    sine = sin_ref[...]
    lanes = lane_ids((rows, 128))

    def window(first):
        return pltpu.roll(whole, (width - first) % width, 1)[:, :128]

    def rotated(first):
        here = window(first)
        ahead = window(first + 48)
        behind = window((first - 48) % width)
        return here * cosine + jnp.where(lanes < 48, ahead, behind) * sine

    def plain(first):
        return jnp.where(lanes < HD, window(first), 0.0)

    key_values = pack_heads(rotated(96), plain(192), rotated(384), plain(480))
    for i in range(3):
        kv_ref[:, 128 * i : 128 * i + 128] = key_values[i].astype(jnp.bfloat16)
    q_ref[:, :128] = rotated(0).astype(jnp.bfloat16)
    q_ref[:, 128:] = rotated(288)[:, :HD].astype(jnp.bfloat16)


def attention(
    info_ref,
    table_ref,
    q_ref,
    ends_ref,
    kv_hbm,
    blank_ref,
    out_hbm,
    kv_ref,
    qs,
    scores,
    peaks,
    totals,
    contexts,
    outs,
    pages,
    kv_sems,
    page_sem,
    out_sem,
):
    group, member, column = info_ref[0], info_ref[1], info_ref[2]
    groups = kv_ref.shape[0]
    rows = MESH_Y * KEYS
    chunk = 256
    targets = outs.shape[0]
    long_planes = 11 * groups * PAIR // 16

    def fetch(k):
        return pltpu.make_async_copy(kv_hbm.at[k], kv_ref.at[k], kv_sems.at[k])

    least = jnp.where(group * PAIR < long_planes, 0, group - 1)

    def start_fetch(k, carry):
        fetch(k).start()
        return carry

    def wait_fetch(k, carry):
        fetch(k).wait()
        return carry

    lax.fori_loop(least, group + 1, start_fetch, 0)

    def send_page(i, carry):
        k = i // targets
        t = i % targets
        page = table_ref[i]
        there = pages.at[t, pl.ds(pl.multiple_of(k * CAP, CAP), CAP), :]

        @pl.when(page >= 0)
        def _():
            first = pl.multiple_of(jnp.maximum(page, 0) * CAP, CAP)
            pltpu.make_async_copy(kv_hbm.at[k, pl.ds(first, CAP), :], there, page_sem).start()

        @pl.when(page < 0)
        def _():
            pltpu.make_async_copy(blank_ref, there, page_sem).start()

        return carry

    lax.fori_loop(0, groups * targets, send_page, 0)

    key_cols = (slice(0, 128), slice(128, 384))
    value_cols = (slice(0, 256), slice(256, 384))
    value_width = (256, 128)
    parts = [
        (head, slice(first, first + chunk), first)
        for head in range(2)
        for first in range(0, rows, chunk)
    ]
    lanes = lane_ids((chunk, 128))

    def one_plane(h, waits):
        plane = group * PAIR + h
        is_long = plane < long_planes
        low = jnp.where(is_long, 0, group - 1)
        masked_low = jnp.where(is_long, group, group - 1)
        count = group + 1 - low

        for first in range(0, rows, chunk):
            start = h * rows + first
            if not isinstance(start, int):
                start = pl.multiple_of(start, chunk)
            here = pl.ds(start, chunk)
            q1 = q_ref[here, 128 : 128 + HD].astype(jnp.float32)
            q1 = jnp.concatenate([q1, jnp.zeros((chunk, 128 - HD), jnp.float32)], axis=1)
            q1 = pltpu.roll(q1, 64, 1)
            span = slice(first, first + chunk)
            qs[span, :128] = q_ref[here, :128]
            qs[span, 128:256] = jnp.where(lanes < 64, 0.0, q1).astype(jnp.bfloat16)
            qs[span, 256:] = jnp.where(lanes < 32, q1, 0.0).astype(jnp.bfloat16)

        peaks[...] = jnp.full_like(peaks, neg_large)
        totals[...] = jnp.zeros_like(totals)
        contexts[...] = jnp.zeros_like(contexts)

        if waits:
            lax.fori_loop(least, group + 1, wait_fetch, 0)

        def score(k, masked):
            for head, span, first in parts:
                s = lax.dot_general(
                    qs[span, key_cols[head]],
                    kv_ref[k, :, key_cols[head]],
                    (((1,), (1,)), ((), ())),
                    preferred_element_type=jnp.float32,
                )
                if masked:
                    shape = (chunk, KEYS)
                    row_ids = plane * rows + first + lax.broadcasted_iota(jnp.int32, shape, 0)
                    key_ids = (
                        (k * PAIR + member) * rows
                        + column * KEYS
                        + lax.broadcasted_iota(jnp.int32, shape, 1)
                    )
                    allowed = (key_ids <= row_ids) & (row_ids < ends_ref[pl.ds(k, 1), :])
                    s = jnp.where(allowed, s, neg_large)
                scores[k - low, head, span, :] = s
                peaks[head, span, :] = jnp.maximum(
                    peaks[head, span, :], jnp.maximum(s[:, :128], s[:, 128:])
                )

        def free_step(k, carry):
            score(k, False)
            return carry

        def masked_step(k, carry):
            score(k, True)
            return carry

        lax.fori_loop(low, masked_low, free_step, 0)
        lax.fori_loop(masked_low, group + 1, masked_step, 0)

        @pl.when(count % 2 == 1)
        def _():
            scores[count] = jnp.full(scores.shape[1:], neg_large, jnp.float32)

        tops = []
        for head, span, first in parts:
            top = jnp.max(peaks[head, span, :], axis=1, keepdims=True)
            tops.append(top)
            peaks[head, span, :] = jnp.broadcast_to(top * log2_scale, (chunk, 128))

        def weigh(i, carry):
            for head, span, first in parts:
                shift = peaks[head, span, :]
                total = totals[head, span, :]
                context = contexts[head, span, : value_width[head]]
                for n in range(2):
                    slot = 2 * i + n
                    k = jnp.minimum(low + slot, group)
                    s = scores[slot, head, span, :]
                    left = jnp.exp2(s[:, :128] * log2_scale - shift)
                    right = jnp.exp2(s[:, 128:] * log2_scale - shift)
                    total = total + (left + right)
                    p = jnp.concatenate(
                        [left.astype(jnp.bfloat16), right.astype(jnp.bfloat16)], axis=1
                    )
                    context = context + jnp.dot(
                        p, kv_ref[k, :, value_cols[head]], preferred_element_type=jnp.float32
                    )
                totals[head, span, :] = total
                contexts[head, span, : value_width[head]] = context
            return carry

        lax.fori_loop(0, (count + 1) // 2, weigh, 0)

        for (head, span, first), top in zip(parts, tops):
            denominator = jnp.sum(totals[head, span, :], axis=1, keepdims=True)
            if head == 0:
                left = pltpu.roll(contexts[head, span, :128], 32, 1)
                right = pltpu.roll(contexts[head, span, 128:], 32, 1)
                context = jnp.where(lanes < 32, left, right)
            else:
                context = pltpu.roll(contexts[head, span, :128], 96, 1)
            context = context / denominator
            lse = top * score_scale + jnp.log(denominator)
            coarse = lse.astype(jnp.bfloat16).astype(jnp.float32)
            middle = (lse - coarse).astype(jnp.bfloat16).astype(jnp.float32)
            fine = lse - coarse - middle
            tail = jnp.where(lanes == HD, coarse, jnp.where(lanes == HD + 1, middle, fine))
            outs[h * MESH_Y + first // KEYS, :, head * 128 : head * 128 + 128] = jnp.where(
                lanes < HD, context, tail
            ).astype(jnp.bfloat16)

    page_rows = groups * CAP
    for h in range(PAIR):
        one_plane(h, h == 0)

    pltpu.make_async_copy(pages, pages, page_sem).wait()
    sends = [
        pltpu.make_async_copy(pages, out_hbm.at[:, pl.ds(0, page_rows), :], page_sem),
        pltpu.make_async_copy(
            outs, out_hbm.at[:, pl.ds(page_rows, KEYS), pl.ds(0, 256)], out_sem
        ),
    ]
    for send in sends:
        send.start()
    for send in sends:
        send.wait()


def combine(
    flag_ref, pages_hbm, got_hbm, att_ref, lse_ref, cache_ref, parts_ref, pages_ref, parts_sem, pages_sem
):
    count = parts_ref.shape[0]
    groups = cache_ref.shape[0]
    load = pltpu.make_async_copy(
        got_hbm.at[:, pl.ds(groups * CAP, KEYS), pl.ds(0, 256)], parts_ref, parts_sem
    )
    load.start()
    load_pages = pltpu.make_async_copy(pages_hbm.at[:, pl.ds(0, groups)], pages_ref, pages_sem)
    load_pages.start()
    load.wait()
    live = flag_ref[0] == 0
    for head in range(2):
        parts = [
            parts_ref[i, :, head * 128 : head * 128 + 128].astype(jnp.float32)
            for i in range(count)
        ]
        lses = [p[:, 96:97] + p[:, 97:98] + p[:, 98:99] for p in parts]
        peak = functools.reduce(jnp.maximum, lses)
        weights = [jnp.exp(v - peak) for v in lses]
        total = functools.reduce(jnp.add, weights)
        context = functools.reduce(jnp.add, [p * w for p, w in zip(parts, weights)])
        lanes = lane_ids(context.shape)
        whole = jnp.where(lanes < HD, context / total, peak + jnp.log(total))
        turned = jnp.where(live, jnp.transpose(whole, (1, 0)), 0.0)
        att_ref[head * HD : head * HD + HD, :] = turned[:HD].astype(jnp.bfloat16)
        lse_ref[head : head + 1, :] = turned[HD : HD + 1]
    load_pages.wait()
    for t in range(count):
        cache_ref[:, t] = pages_ref[t]


SMEM = pl.BlockSpec(memory_space=pltpu.SMEM)
VMEM = pl.BlockSpec(memory_space=pltpu.VMEM)
ANY = pl.BlockSpec(memory_space=pl.ANY)
SMALL = pltpu.CompilerParams(vmem_limit_bytes=40 << 20)


def in_vmem(x):
    return pltpu.with_memory_space_constraint(x, pltpu.VMEM)


def in_hbm(x):
    return pltpu.with_memory_space_constraint(x, pltpu.HBM)


def body(stream_x, qkv_weight, short_lengths, cache_owner):
    groups, columns = lax.axis_size("q"), lax.axis_size("y")
    targets = PAIR * columns
    tok_count = stream_x.shape[0]
    group, member, column = lax.axis_index("q"), lax.axis_index("p"), lax.axis_index("y")
    plane = group * PAIR + member
    core = lax.axis_index("c").astype(jnp.int32).reshape(1)
    plane_rows = tok_count * columns
    long_planes = groups * PAIR * 11 // 16
    bounds = boundaries(short_lengths, plane_rows * long_planes)

    weight = in_vmem(qkv_weight.T)
    ours = lax.all_gather(stream_x, "x", axis=0, tiled=True)
    theirs = lax.ppermute(ours, "c", [(0, 1), (1, 0)])

    row_ids = (
        plane * plane_rows + column * tok_count + jnp.arange(tok_count, dtype=jnp.int32)
    )
    passed = row_ids[:, None] >= bounds[None, :]
    seg_begin = jnp.max(jnp.where(passed, bounds[None, :], 0), axis=1)
    position = (row_ids - seg_begin).astype(jnp.float32)
    half_dim = HD // 2
    lane = jnp.arange(128, dtype=jnp.int32)
    entry = jnp.where(lane < half_dim, lane, lane - half_dim)
    inverse_freq = rope_base ** (-entry.astype(jnp.float32) / half_dim)
    sign = jnp.where(lane < half_dim, -1.0, jnp.where(lane < HD, 1.0, 0.0))
    angle = position[:, None] * inverse_freq[None, :]
    cosine = jnp.where(lane[None, :] < HD, jnp.cos(angle), 0.0)
    sine = jnp.sin(angle) * sign[None, :]

    half = pl.pallas_call(
        half_projection,
        in_specs=[SMEM, VMEM, VMEM],
        out_specs=VMEM,
        out_shape=jax.ShapeDtypeStruct((tok_count, qkv_weight.shape[1]), jnp.float32),
        compiler_params=SMALL,
    )(core, in_vmem(ours), weight)
    queries, key_values = pl.pallas_call(
        rest_projection,
        in_specs=[SMEM] + [VMEM] * 5,
        out_specs=[VMEM, VMEM],
        out_shape=[
            jax.ShapeDtypeStruct((tok_count, 128 + HD), jnp.bfloat16),
            jax.ShapeDtypeStruct((tok_count, 384), jnp.bfloat16),
        ],
        compiler_params=SMALL,
    )(1 - core, in_vmem(theirs), weight, in_vmem(half), in_vmem(cosine), in_vmem(sine))

    gathered = lax.all_gather(key_values, "q", axis=0, tiled=True)
    queries, short_lengths, cache_owner = lax.optimization_barrier(
        (queries, short_lengths, cache_owner)
    )
    plane_queries = lax.all_gather(queries, ("p", "y"), axis=0, tiled=True)

    bounds = boundaries(short_lengths, plane_rows * long_planes)
    key_ids = (
        (jnp.arange(groups, dtype=jnp.int32) * PAIR + member) * plane_rows + column * tok_count
    )[:, None] + jnp.arange(tok_count, dtype=jnp.int32)[None, :]
    ends = jnp.min(
        jnp.where(bounds[None, None, :] > key_ids[:, :, None], bounds[None, None, :], 1 << 30),
        axis=2,
    )

    pages = tok_count // CAP
    owners = groups * PAIR * columns
    page_owner = cache_owner.reshape(pages, CAP)[:, 0]
    page_live = row_ids.reshape(pages, CAP)[:, 0] < bounds[-1]
    hit = (page_owner[:, None] == jnp.arange(owners, dtype=jnp.int32)[None, :]) & page_live[:, None]
    page_map = jnp.max(jnp.where(hit, jnp.arange(pages, dtype=jnp.int32)[:, None], -1), axis=0)
    maps = lax.all_gather(page_map[None, :], "q", axis=0, tiled=True)
    table = lax.dynamic_slice_in_dim(maps, group * targets, targets, 1).reshape(-1)
    info = jnp.stack([group, member, column]).astype(jnp.int32)
    blank = jnp.zeros((CAP, 384), jnp.bfloat16)
    gathered, plane_queries, ends, table, info, blank = lax.optimization_barrier(
        (gathered, plane_queries, ends, table, info, blank)
    )

    most = max((long_planes - 1) // PAIR + 1, 2)
    slots = 2 * ((most + 1) // 2)
    page_rows = groups * CAP
    outbox = pl.pallas_call(
        attention,
        in_specs=[SMEM, SMEM, VMEM, VMEM, ANY, VMEM],
        out_specs=ANY,
        out_shape=jax.ShapeDtypeStruct((targets, page_rows + tok_count, 384), jnp.bfloat16),
        scratch_shapes=[
            pltpu.VMEM((groups, tok_count, 384), jnp.bfloat16),
            pltpu.VMEM((plane_rows, 384), jnp.bfloat16),
            pltpu.VMEM((slots, 2, plane_rows, 256), jnp.float32),
            pltpu.VMEM((2, plane_rows, 128), jnp.float32),
            pltpu.VMEM((2, plane_rows, 128), jnp.float32),
            pltpu.VMEM((2, plane_rows, 256), jnp.float32),
            pltpu.VMEM((targets, tok_count, 256), jnp.bfloat16),
            pltpu.VMEM((targets, page_rows, 384), jnp.bfloat16),
            pltpu.SemaphoreType.DMA((groups,)),
            pltpu.SemaphoreType.DMA,
            pltpu.SemaphoreType.DMA,
        ],
    )(info, table, plane_queries, ends, gathered.reshape(groups, tok_count, 384), blank)
    received = lax.all_to_all(outbox, ("p", "y"), split_axis=0, concat_axis=0, tiled=True)
    padding = (row_ids[:1] >= bounds[-1]).astype(jnp.int32)
    attended, row_lse, kv_cache = pl.pallas_call(
        combine,
        in_specs=[SMEM, ANY, ANY],
        out_specs=[VMEM, VMEM, VMEM],
        out_shape=[
            jax.ShapeDtypeStruct((2 * HD, tok_count), jnp.bfloat16),
            jax.ShapeDtypeStruct((2, tok_count), jnp.float32),
            jax.ShapeDtypeStruct((groups, targets, CAP, 384), jnp.bfloat16),
        ],
        scratch_shapes=[
            pltpu.VMEM((targets, tok_count, 256), jnp.bfloat16),
            pltpu.VMEM((targets, groups, CAP, 384), jnp.bfloat16),
            pltpu.SemaphoreType.DMA,
            pltpu.SemaphoreType.DMA,
        ],
    )(
        padding,
        received.reshape(targets, (page_rows + tok_count) // CAP, CAP, 384),
        received,
    )
    return (attended.T, row_lse, kv_cache.reshape(-1, 384))


def solution(mesh):
    seq, head = mesh.devices.shape
    shape = (seq // (MESH_Y * PAIR), PAIR, MESH_Y, head // 2, 2)
    fine = Mesh(mesh.devices.reshape(shape), ("q", "p", "y", "x", "c"))
    seq_axes, head_axes = ("q", "p", "y"), ("x", "c")
    return jax.shard_map(
        body,
        mesh=fine,
        in_specs=(P(seq_axes, head_axes), P(None, head_axes), P(), P(seq_axes, None)),
        out_specs=(P(seq_axes, head_axes), P(head_axes, seq_axes), P(seq_axes, head_axes)),
        check_vma=False,
    )
```

profile of v0, /device:TPU:6, one launch (start us, length us, event | category | flops | bytes accessed | tf_op | source)
XLA Modules:
  0.0 150.2 jit_solution(11464429491172515085)
XLA Ops:
  7.2 0.0 all-gather.3.cloned.1.call-start
  7.2 16.2 %all_gather.12.x_ref = bf16[1024,384]{1,0:T(8,128)(2,1)S(1)} all-gather(bf16[256,384]{1,0:T(8,128)(2,1)} %param.4), channel_id=1, replica_groups=mesh['q'=8,'p'=2,'y'=4,'x'=4,'c'=2] {'x'}, dimensions={0}, use_global_device_ids=true | all-gather | bytes 983040 | tf_op jit(solution)/shard_map/all_gather | solution.py:354
  23.4 1.9 %collective-permute-start = (bf16[1024,384]{1,0:T(8,128)(2,1)S(1)}, bf16[1024,384]{1,0:T(8,128)(2,1)S(1)}, u32[]{:S(2)}, u32[]{:S(2)}) collective-permute-start(bf16[1024,384]{1,0:T(8,128)(2,1)S(1)} %all_gather.12.x_ref), channel_id=1, source_target_pairs={{0,1},{1,0},{2,3},{3,2},{4,5},{5,4},{6,7},{7,6},{8,9},{9,8},{10,11... | collective-permute-start | bytes 2359304 | tf_op jit(solution)/shard_map/ppermute | solution.py:355
  25.4 0.7 select_reduce_fusion.4
  26.1 0.0 copy-start
  26.1 2.0 %copy-done = bf16[3072,576]{0,1:T(8,128)(2,1)S(1)} copy-done((bf16[3072,576]{0,1:T(8,128)(2,1)S(1)}, bf16[3072,576]{0,1:T(8,128)(2,1)}, u32[]{:S(2)}) %copy-start) | copy-done | bytes 3538968
  28.1 0.0 copy-start.1
  28.1 1.0 shard_map.67.first_ref
  29.2 0.1 select_reduce_fusion.1
  29.3 0.5 fusion.1
  29.8 0.0 collective-permute-done.x_ref
  29.8 0.3 copy-done.1
  30.1 0.0 copy-start.4
  30.1 0.0 copy-start.3
  30.1 2.4 %shard_map.68 = (bf16[256,224]{1,0:T(8,128)(2,1)S(1)}, bf16[256,384]{1,0:T(8,128)(2,1)}) custom-call(s32[1]{0:T(128)S(6)} %sub.13.core_ref, bf16[1024,384]{1,0:T(8,128)(2,1)S(1)} %collective-permute-done.x_ref, bf16[576,3072]{1,0:T(8,128)(2,1)S(1)} %bitcast.15, f32[256,576]{1,0:T(8,128)S(1)} %shard_map.67.first_ref, ...), custom_call_target="tpu_custom_call" | custom-call | tf_op jit(solution)/shard_map/pallas_call | solution.py:379
  32.5 0.0 all-gather.3.cloned.1.call-update
  32.5 1.2 dynamic-slice
  34.3 0.7 pad_add_fusion.info_ref
  35.0 0.1 iota_add_fusion
  35.1 0.0 copy-done.4
  35.1 0.1 select_reduce_fusion.3
  35.2 0.6 slice.14
  35.8 0.5 broadcast.122
  36.3 0.0 copy-done.3
  36.3 0.7 reduce.5
  36.9 0.1 reshape.94
  37.0 0.1 slice_reduce_fusion
  37.1 0.6 compare_bitcast_fusion
  37.7 0.1 select_reduce_fusion.2
  37.8 0.2 dynamic-update-slice
  38.1 0.1 reshape.99
  38.1 22.9 %all-reduce.1 = s32[8,64]{1,0:T(8,128)S(1)} all-reduce(s32[8,64]{1,0:T(8,128)S(1)} %reshape.99), channel_id=2, replica_groups=mesh['q'=8,'p'=2,'y'=4,'x'=4,'c'=2] {'q'}, use_global_device_ids=true, to_apply=%add | all-reduce | flops 512 | bytes 4096
  61.0 0.1 constant_dynamic-slice_fusion
  61.1 0.6 reshape.95.table_ref
  61.7 0.7 select_reduce_fusion.ends_ref
  62.4 39.6 %all_gather.14.q_ref = bf16[2048,224]{1,0:T(8,128)(2,1)} all-gather(bf16[256,224]{1,0:T(8,128)(2,1)S(1)} %get-tuple-element.20), channel_id=1, replica_groups=mesh['q'=8,'p'=2,'y'=4,'x'=4,'c'=2] {'p','y'}, dimensions={0}, use_global_device_ids=true | all-gather | bytes 1032192 | tf_op jit(solution)/shard_map/all_gather | solution.py:394
  102.0 0.0 all-gather.3.cloned.1.call-done
  102.0 0.6 broadcast_in_dim.114.blank_ref
  102.6 10.2 %shard_map.69 = bf16[8,320,384]{2,1,0:T(8,128)(2,1)} custom-call(s32[3]{0:T(128)} %pad_add_fusion.info_ref, s32[64]{0:T(128)} %reshape.95.table_ref, bf16[2048,224]{1,0:T(8,128)(2,1)} %all_gather.14.q_ref, s32[8,256]{1,0:T(8,128)} %select_reduce_fusion.ends_ref, bf16[8,256,384]{2,1,0:T(8,128)(2,1)} %bitcast.17, bf16[8,384]{1,0:T(8,128)(2,1)} %broadcast_in_dim.114.blank_ref), custom_call_target="tpu_custom_call" | custom-call | tf_op jit(solution)/shard_map/pallas_call | solution.py:422
  112.8 3.7 %all-to-all-start = ((bf16[8,320,384]{2,1,0:T(8,128)(2,1)}), bf16[8,320,384]{2,1,0:T(8,128)(2,1)S(1)}, u32[]{:S(2)}, u32[]{:S(2)}) async-start(bf16[8,320,384]{2,1,0:T(8,128)(2,1)} %shard_map.69), calls=%async_computation | async-start | bytes 3932160 | tf_op jit(solution)/shard_map/all_to_all | solution.py:441
  116.4 0.5 slice.13
  118.2 20.2 %all-to-all-done.got_hbm = bf16[8,320,384]{2,1,0:T(8,128)(2,1)S(1)} async-done(((bf16[8,320,384]{2,1,0:T(8,128)(2,1)}), bf16[8,320,384]{2,1,0:T(8,128)(2,1)S(1)}, u32[]{:S(2)}, u32[]{:S(2)}) %all-to-all-start) | async-done | bytes 1966112 | tf_op jit(solution)/shard_map/all_to_all | solution.py:441
  138.3 0.0 copy-start.2
  138.3 1.3 copy-done.2
  139.6 3.7 %shard_map.70 = (bf16[192,256]{1,0:T(8,128)(2,1)}, f32[2,256]{1,0:T(2,128)}, bf16[8,8,8,384]{3,2,1,0:T(8,128)(2,1)}) custom-call(s32[1]{0:T(128)S(6)} %convert_element_type.19.flag_ref, bf16[8,40,8,384]{3,2,1,0:T(8,128)(2,1)} %bitcast.16, bf16[8,320,384]{2,1,0:T(8,128)(2,1)} %copy-done.2), custom_call_target="tpu_custom_call" | custom-call | tf_op jit(solution)/shard_map/pallas_call | solution.py:443
  (9 shorter events, 0.1 us)
Async XLA Ops:
  7.2 94.8 %all-gather.3.cloned.1.call-start = ((), (), s32[]{:S(2)}) async-start(), calls=%async_computation.1 | async-start | bytes 1769472 | tf_op jit(solution)/shard_map/all_gather | solution.py:390
  23.4 6.4 %collective-permute-start = (bf16[1024,384]{1,0:T(8,128)(2,1)S(1)}, bf16[1024,384]{1,0:T(8,128)(2,1)S(1)}, u32[]{:S(2)}, u32[]{:S(2)}) collective-permute-start(bf16[1024,384]{1,0:T(8,128)(2,1)S(1)} %all_gather.12.x_ref), channel_id=1, source_target_pairs={{0,1},{1,0},{2,3},{3,2},{4,5},{5,4},{6,7},{7,6},{8,9},{9,8},{10,11... | collective-permute-start | bytes 2359304 | tf_op jit(solution)/shard_map/ppermute | solution.py:355
  26.1 2.0 %copy-start = (bf16[3072,576]{0,1:T(8,128)(2,1)S(1)}, bf16[3072,576]{0,1:T(8,128)(2,1)}, u32[]{:S(2)}) copy-start(bf16[3072,576]{0,1:T(8,128)(2,1)} %param.5) | copy-start | bytes 10616836
  28.1 2.0 %copy-start.1 = (bf16[3072,576]{0,1:T(8,128)(2,1)S(1)}, bf16[3072,576]{0,1:T(8,128)(2,1)}, u32[]{:S(2)}) copy-start(bf16[3072,576]{0,1:T(8,128)(2,1)} %param.5) | copy-start | bytes 10616836
  30.1 5.0 %copy-start.4 = (s32[32]{0:T(128)S(1)}, s32[32]{0:T(128)}, u32[]{:S(2)}) copy-start(s32[32]{0:T(128)} %param.6) | copy-start | bytes 388
  30.1 6.1 %copy-start.3 = (s32[256,1]{0,1:T(1,128)S(1)}, s32[256,1]{0,1:T(1,128)}, u32[]{:S(2)}) copy-start(s32[256,1]{0,1:T(1,128)} %param.7) | copy-start | bytes 3076
  112.8 25.6 %all-to-all-start = ((bf16[8,320,384]{2,1,0:T(8,128)(2,1)}), bf16[8,320,384]{2,1,0:T(8,128)(2,1)S(1)}, u32[]{:S(2)}, u32[]{:S(2)}) async-start(bf16[8,320,384]{2,1,0:T(8,128)(2,1)} %shard_map.69), calls=%async_computation | async-start | bytes 3932160 | tf_op jit(solution)/shard_map/all_to_all | solution.py:441
  138.3 1.3 copy-start.2
Sparse Core Ops, SparseCore 0:
  32.6 66.6 all-gather.2
where the time goes:
time: 151 us; the launch traced here: 150 us
  blocking collectives  78.6 us (52%)
  waiting for transfers between devices  20.2 us (13%)
  Pallas kernels  17.2 us (11%)
  between operations  16 us (11%)
  local copies, waits for them, and re-layouts  8.23 us (5%)
  starting transfers between devices  5.63 us (4%)
  other arithmetic  4.28 us (3%)
    all_gather x1, blocking collectives, body(): plane_queries = lax.all_gather(queries, ('p', 'y'), axis=0, tiled=True)  39.6 us
    unnamed x1, blocking collectives  22.9 us
    all_to_all x1, waiting for transfers between devices, body(): lax.all_to_all(outbox, ('p', 'y'), split_axis=0, concat_axis=0, tiled=True)  20.2 us
    all_gather x1, blocking collectives, body(): ours = lax.all_gather(stream_x, 'x', axis=0, tiled=True)  16.2 us
    pallas_call x1, Pallas kernels, body(): pl.pallas_call(attention, in_specs=[SMEM, SMEM, VMEM, VMEM, ANY, VMEM], o...  10.2 us
    unnamed x13, local copies, waits for them, and re-layouts  5.08 us
    pallas_call x1, Pallas kernels, body(): pl.pallas_call(combine, in_specs=[SMEM, ANY, ANY], out_specs=[VMEM, VMEM,...  3.69 us
    all_to_all x1, starting transfers between devices, body(): lax.all_to_all(outbox, ('p', 'y'), split_axis=0, concat_axis=0, tiled=True)  3.68 us
  transfers between devices with their start and end apart: 3, of which 1 were waited for; matrix products, arithmetic and copies ran while one was open for 6% of the time, Pallas kernels for 1%

commit v1 on v0

--- a/solution.py
+++ b/solution.py
@@ -63,7 +63,9 @@
     )
 
 
-def rest_projection(core_ref, x_ref, w_ref, first_ref, cos_ref, sin_ref, q_ref, kv_ref):
+def rest_projection(
+    core_ref, x_ref, w_ref, first_ref, cos_ref, sin_ref, owner_ref, q_ref, kv_ref
+):
     total = first_ref[...] + block_sum(core_ref[0], x_ref, w_ref)
     rows, columns = total.shape
     width = columns + 64
@@ -86,36 +88,23 @@
 
     key_values = pack_heads(rotated(96), plain(192), rotated(384), plain(480))
     for i in range(3):
-        kv_ref[:, 128 * i : 128 * i + 128] = key_values[i].astype(jnp.bfloat16)
+        kv_ref[:rows, 128 * i : 128 * i + 128] = key_values[i].astype(jnp.bfloat16)
+    extra = kv_ref.shape[0] - rows
+    kv_ref[rows:, :rows] = jnp.broadcast_to(owner_ref[...], (extra, rows)).astype(jnp.bfloat16)
+    kv_ref[rows:, rows:] = jnp.zeros((extra, 384 - rows), jnp.bfloat16)
     q_ref[:, :128] = rotated(0).astype(jnp.bfloat16)
     q_ref[:, 128:] = rotated(288)[:, :HD].astype(jnp.bfloat16)
 
 
 def attention(
-    info_ref,
-    table_ref,
-    q_ref,
-    ends_ref,
-    kv_hbm,
-    blank_ref,
-    out_hbm,
-    kv_ref,
-    qs,
-    scores,
-    peaks,
-    totals,
-    contexts,
-    outs,
-    pages,
-    kv_sems,
-    page_sem,
-    out_sem,
+    info_ref, q_ref, ends_ref, kv_hbm, out_ref, kv_ref, qs, scores, peaks, totals, contexts, kv_sems
 ):
     group, member, column = info_ref[0], info_ref[1], info_ref[2]
     groups = kv_ref.shape[0]
     rows = MESH_Y * KEYS
     chunk = 256
-    targets = outs.shape[0]
+    targets = out_ref.shape[0]
+    page_rows = groups * CAP
     long_planes = 11 * groups * PAIR // 16
 
     def fetch(k):
@@ -132,25 +121,8 @@
         return carry
 
     lax.fori_loop(least, group + 1, start_fetch, 0)
-
-    def send_page(i, carry):
-        k = i // targets
-        t = i % targets
-        page = table_ref[i]
-        there = pages.at[t, pl.ds(pl.multiple_of(k * CAP, CAP), CAP), :]
-
-        @pl.when(page >= 0)
-        def _():
-            first = pl.multiple_of(jnp.maximum(page, 0) * CAP, CAP)
-            pltpu.make_async_copy(kv_hbm.at[k, pl.ds(first, CAP), :], there, page_sem).start()
-
-        @pl.when(page < 0)
-        def _():
-            pltpu.make_async_copy(blank_ref, there, page_sem).start()
-
-        return carry
-
-    lax.fori_loop(0, groups * targets, send_page, 0)
+    lax.fori_loop(0, least, start_fetch, 0)
+    lax.fori_loop(group + 1, groups, start_fetch, 0)
 
     key_cols = (slice(0, 128), slice(128, 384))
     value_cols = (slice(0, 256), slice(256, 384))
@@ -193,7 +165,7 @@
             for head, span, first in parts:
                 s = lax.dot_general(
                     qs[span, key_cols[head]],
-                    kv_ref[k, :, key_cols[head]],
+                    kv_ref[k, :KEYS, key_cols[head]],
                     (((1,), (1,)), ((), ())),
                     preferred_element_type=jnp.float32,
                 )
@@ -249,7 +221,7 @@
                         [left.astype(jnp.bfloat16), right.astype(jnp.bfloat16)], axis=1
                     )
                     context = context + jnp.dot(
-                        p, kv_ref[k, :, value_cols[head]], preferred_element_type=jnp.float32
+                        p, kv_ref[k, :KEYS, value_cols[head]], preferred_element_type=jnp.float32
                     )
                 totals[head, span, :] = total
                 contexts[head, span, : value_width[head]] = context
@@ -257,39 +229,64 @@
 
         lax.fori_loop(0, (count + 1) // 2, weigh, 0)
 
-        for (head, span, first), top in zip(parts, tops):
-            denominator = jnp.sum(totals[head, span, :], axis=1, keepdims=True)
-            if head == 0:
-                left = pltpu.roll(contexts[head, span, :128], 32, 1)
-                right = pltpu.roll(contexts[head, span, 128:], 32, 1)
-                context = jnp.where(lanes < 32, left, right)
-            else:
-                context = pltpu.roll(contexts[head, span, :128], 96, 1)
-            context = context / denominator
-            lse = top * score_scale + jnp.log(denominator)
-            coarse = lse.astype(jnp.bfloat16).astype(jnp.float32)
-            middle = (lse - coarse).astype(jnp.bfloat16).astype(jnp.float32)
-            fine = lse - coarse - middle
-            tail = jnp.where(lanes == HD, coarse, jnp.where(lanes == HD + 1, middle, fine))
-            outs[h * MESH_Y + first // KEYS, :, head * 128 : head * 128 + 128] = jnp.where(
-                lanes < HD, context, tail
-            ).astype(jnp.bfloat16)
-
-    page_rows = groups * CAP
+        for first in range(0, rows, chunk):
+            span = slice(first, first + chunk)
+            found = []
+            columns = []
+            for head in range(2):
+                top = tops[head * (rows // chunk) + first // chunk]
+                denominator = jnp.sum(totals[head, span, :], axis=1, keepdims=True)
+                if head == 0:
+                    left = pltpu.roll(contexts[head, span, :128], 32, 1)
+                    right = pltpu.roll(contexts[head, span, 128:], 32, 1)
+                    context = jnp.where(lanes < 32, left, right)
+                else:
+                    context = pltpu.roll(contexts[head, span, :128], 96, 1)
+                found.append(jnp.where(lanes < HD, context / denominator, 0.0))
+                lse = top * score_scale + jnp.log(denominator)
+                coarse = lse.astype(jnp.bfloat16).astype(jnp.float32)
+                middle = (lse - coarse).astype(jnp.bfloat16).astype(jnp.float32)
+                columns += [coarse, middle, lse - coarse - middle]
+            target = h * MESH_Y + first // KEYS
+            mid = chunk // 2
+            packed = pack_heads(found[0][:mid], found[1][:mid], found[0][mid:], found[1][mid:])
+            for i in range(3):
+                out_ref[target, page_rows : page_rows + mid, 128 * i : 128 * i + 128] = packed[
+                    i
+                ].astype(jnp.bfloat16)
+            spread = jnp.zeros((chunk, 128), jnp.float32)
+            for i, value in enumerate(columns):
+                spread = jnp.where(lanes == i, value, spread)
+            tail = slice(page_rows + mid, page_rows + mid + 16)
+            out_ref[target, tail, :chunk] = jnp.transpose(spread, (1, 0))[:16].astype(jnp.bfloat16)
+            out_ref[target, tail, chunk:] = jnp.zeros((16, 384 - chunk), jnp.bfloat16)
+
     for h in range(PAIR):
         one_plane(h, h == 0)
 
-    pltpu.make_async_copy(pages, pages, page_sem).wait()
-    sends = [
-        pltpu.make_async_copy(pages, out_hbm.at[:, pl.ds(0, page_rows), :], page_sem),
-        pltpu.make_async_copy(
-            outs, out_hbm.at[:, pl.ds(page_rows, KEYS), pl.ds(0, 256)], out_sem
-        ),
-    ]
-    for send in sends:
-        send.start()
-    for send in sends:
-        send.wait()
+    lax.fori_loop(0, least, wait_fetch, 0)
+    lax.fori_loop(group + 1, groups, wait_fetch, 0)
+    shape = (targets * 16, KEYS)
+    row = lax.broadcasted_iota(jnp.int32, shape, 0)
+    key = lax.broadcasted_iota(jnp.int32, shape, 1)
+    same_place = (row & 7) == (key & 7)
+    parity = (row >> 3) & 1
+    owner = (group * targets + (row >> 4)).astype(jnp.float32)
+    for two in range(groups // 2):
+        total = None
+        for n in range(2):
+            k = 2 * two + n
+            owners = kv_ref[k, KEYS : KEYS + 16, :KEYS].astype(jnp.float32)[:1]
+            chosen = (owners == owner) & same_place & (parity == n)
+            picked = jnp.dot(
+                jnp.where(chosen, 1.0, 0.0).astype(jnp.bfloat16),
+                kv_ref[k, :KEYS, :],
+                preferred_element_type=jnp.float32,
+            )
+            total = picked if total is None else total + picked
+        total = total.astype(jnp.bfloat16)
+        for t in range(targets):
+            out_ref[t, 16 * two : 16 * two + 16, :] = total[16 * t : 16 * t + 16]
 
 
 def combine(
@@ -298,28 +295,51 @@
     count = parts_ref.shape[0]
     groups = cache_ref.shape[0]
     load = pltpu.make_async_copy(
-        got_hbm.at[:, pl.ds(groups * CAP, KEYS), pl.ds(0, 256)], parts_ref, parts_sem
+        got_hbm.at[:, pl.ds(groups * CAP, parts_ref.shape[1]), :], parts_ref, parts_sem
     )
     load.start()
     load_pages = pltpu.make_async_copy(pages_hbm.at[:, pl.ds(0, groups)], pages_ref, pages_sem)
     load_pages.start()
     load.wait()
     live = flag_ref[0] == 0
+    mid = KEYS // 2
+    shares = []
     for head in range(2):
-        parts = [
-            parts_ref[i, :, head * 128 : head * 128 + 128].astype(jnp.float32)
-            for i in range(count)
-        ]
-        lses = [p[:, 96:97] + p[:, 97:98] + p[:, 98:99] for p in parts]
-        peak = functools.reduce(jnp.maximum, lses)
-        weights = [jnp.exp(v - peak) for v in lses]
-        total = functools.reduce(jnp.add, weights)
-        context = functools.reduce(jnp.add, [p * w for p, w in zip(parts, weights)])
-        lanes = lane_ids(context.shape)
-        whole = jnp.where(lanes < HD, context / total, peak + jnp.log(total))
-        turned = jnp.where(live, jnp.transpose(whole, (1, 0)), 0.0)
-        att_ref[head * HD : head * HD + HD, :] = turned[:HD].astype(jnp.bfloat16)
-        lse_ref[head : head + 1, :] = turned[HD : HD + 1]
+        lses = []
+        for i in range(count):
+            rows = parts_ref[i, mid : mid + 16, :KEYS].astype(jnp.float32)
+            first = 3 * head
+            lses.append(
+                rows[first : first + 1] + rows[first + 1 : first + 2] + rows[first + 2 : first + 3]
+            )
+        lses = jnp.concatenate(lses, axis=0)
+        peak = jnp.max(lses, axis=0, keepdims=True)
+        weights = jnp.exp(lses - peak)
+        total = jnp.sum(weights, axis=0, keepdims=True)
+        shares.append(weights / total)
+        lse_ref[head : head + 1, :] = jnp.where(live, peak + jnp.log(total), 0.0)
+    shares.append(jnp.zeros((128 - 2 * count, KEYS), jnp.float32))
+    shares = jnp.transpose(jnp.concatenate(shares, axis=0), (1, 0))
+    lanes = lane_ids((mid, 128))
+    sums = [None] * 3
+    for i in range(count):
+        near0, near1 = shares[:mid, i : i + 1], shares[:mid, count + i : count + i + 1]
+        far0, far1 = shares[mid:, i : i + 1], shares[mid:, count + i : count + i + 1]
+        spread = (
+            jnp.where(lanes < 96, near0, near1),
+            jnp.where(lanes < 64, near1, far0),
+            jnp.where(lanes < 32, far0, far1),
+        )
+        for j in range(3):
+            part = parts_ref[i, :mid, 128 * j : 128 * j + 128].astype(jnp.float32) * spread[j]
+            sums[j] = part if sums[j] is None else sums[j] + part
+    turned = [
+        jnp.where(live, jnp.transpose(v, (1, 0)), 0.0).astype(jnp.bfloat16) for v in sums
+    ]
+    att_ref[:128, :mid] = turned[0]
+    att_ref[128:, :mid] = turned[1][:64]
+    att_ref[:64, mid:] = turned[1][64:]
+    att_ref[64:, mid:] = turned[2]
     load_pages.wait()
     for t in range(count):
         cache_ref[:, t] = pages_ref[t]
@@ -369,6 +389,9 @@
     cosine = jnp.where(lane[None, :] < HD, jnp.cos(angle), 0.0)
     sine = jnp.sin(angle) * sign[None, :]
 
+    owner_row = jnp.where(row_ids < bounds[-1], cache_owner.reshape(tok_count), -1)
+    owner_row = owner_row.astype(jnp.float32)[None, :]
+
     half = pl.pallas_call(
         half_projection,
         in_specs=[SMEM, VMEM, VMEM],
@@ -378,19 +401,17 @@
     )(core, in_vmem(ours), weight)
     queries, key_values = pl.pallas_call(
         rest_projection,
-        in_specs=[SMEM] + [VMEM] * 5,
+        in_specs=[SMEM] + [VMEM] * 6,
         out_specs=[VMEM, VMEM],
         out_shape=[
             jax.ShapeDtypeStruct((tok_count, 128 + HD), jnp.bfloat16),
-            jax.ShapeDtypeStruct((tok_count, 384), jnp.bfloat16),
+            jax.ShapeDtypeStruct((tok_count + 16, 384), jnp.bfloat16),
         ],
         compiler_params=SMALL,
-    )(1 - core, in_vmem(theirs), weight, in_vmem(half), in_vmem(cosine), in_vmem(sine))
+    )(1 - core, in_vmem(theirs), weight, in_vmem(half), in_vmem(cosine), in_vmem(sine), owner_row)
 
     gathered = lax.all_gather(key_values, "q", axis=0, tiled=True)
-    queries, short_lengths, cache_owner = lax.optimization_barrier(
-        (queries, short_lengths, cache_owner)
-    )
+    queries, short_lengths = lax.optimization_barrier((queries, short_lengths))
     plane_queries = lax.all_gather(queries, ("p", "y"), axis=0, tiled=True)
 
     bounds = boundaries(short_lengths, plane_rows * long_planes)
@@ -402,42 +423,30 @@
         axis=2,
     )
 
-    pages = tok_count // CAP
-    owners = groups * PAIR * columns
-    page_owner = cache_owner.reshape(pages, CAP)[:, 0]
-    page_live = row_ids.reshape(pages, CAP)[:, 0] < bounds[-1]
-    hit = (page_owner[:, None] == jnp.arange(owners, dtype=jnp.int32)[None, :]) & page_live[:, None]
-    page_map = jnp.max(jnp.where(hit, jnp.arange(pages, dtype=jnp.int32)[:, None], -1), axis=0)
-    maps = lax.all_gather(page_map[None, :], "q", axis=0, tiled=True)
-    table = lax.dynamic_slice_in_dim(maps, group * targets, targets, 1).reshape(-1)
     info = jnp.stack([group, member, column]).astype(jnp.int32)
-    blank = jnp.zeros((CAP, 384), jnp.bfloat16)
-    gathered, plane_queries, ends, table, info, blank = lax.optimization_barrier(
-        (gathered, plane_queries, ends, table, info, blank)
+    gathered, plane_queries, ends, info = lax.optimization_barrier(
+        (gathered, plane_queries, ends, info)
     )
 
     most = max((long_planes - 1) // PAIR + 1, 2)
     slots = 2 * ((most + 1) // 2)
     page_rows = groups * CAP
+    box_rows = page_rows + tok_count // 2 + 16
     outbox = pl.pallas_call(
         attention,
-        in_specs=[SMEM, SMEM, VMEM, VMEM, ANY, VMEM],
-        out_specs=ANY,
-        out_shape=jax.ShapeDtypeStruct((targets, page_rows + tok_count, 384), jnp.bfloat16),
+        in_specs=[SMEM, VMEM, VMEM, ANY],
+        out_specs=VMEM,
+        out_shape=jax.ShapeDtypeStruct((targets, box_rows, 384), jnp.bfloat16),
         scratch_shapes=[
-            pltpu.VMEM((groups, tok_count, 384), jnp.bfloat16),
+            pltpu.VMEM((groups, tok_count + 16, 384), jnp.bfloat16),
             pltpu.VMEM((plane_rows, 384), jnp.bfloat16),
             pltpu.VMEM((slots, 2, plane_rows, 256), jnp.float32),
             pltpu.VMEM((2, plane_rows, 128), jnp.float32),
             pltpu.VMEM((2, plane_rows, 128), jnp.float32),
             pltpu.VMEM((2, plane_rows, 256), jnp.float32),
-            pltpu.VMEM((targets, tok_count, 256), jnp.bfloat16),
-            pltpu.VMEM((targets, page_rows, 384), jnp.bfloat16),
             pltpu.SemaphoreType.DMA((groups,)),
-            pltpu.SemaphoreType.DMA,
-            pltpu.SemaphoreType.DMA,
         ],
-    )(info, table, plane_queries, ends, gathered.reshape(groups, tok_count, 384), blank)
+    )(info, plane_queries, ends, gathered.reshape(groups, tok_count + 16, 384))
     received = lax.all_to_all(outbox, ("p", "y"), split_axis=0, concat_axis=0, tiled=True)
     padding = (row_ids[:1] >= bounds[-1]).astype(jnp.int32)
     attended, row_lse, kv_cache = pl.pallas_call(
@@ -450,14 +459,14 @@
             jax.ShapeDtypeStruct((groups, targets, CAP, 384), jnp.bfloat16),
         ],
         scratch_shapes=[
-            pltpu.VMEM((targets, tok_count, 256), jnp.bfloat16),
+            pltpu.VMEM((targets, tok_count // 2 + 16, 384), jnp.bfloat16),
             pltpu.VMEM((targets, groups, CAP, 384), jnp.bfloat16),
             pltpu.SemaphoreType.DMA,
             pltpu.SemaphoreType.DMA,
         ],
     )(
         padding,
-        received.reshape(targets, (page_rows + tok_count) // CAP, CAP, 384),
+        received.reshape(targets, box_rows // CAP, CAP, 384),
         received,
     )
     return (attended.T, row_lse, kv_cache.reshape(-1, 384))

time: 151 us -> 141 us (0.934)
  blocking collectives: 78.6 us -> 53.6 us
  waiting for transfers between devices: 20.2 us -> 38.9 us
  local copies, waits for them, and re-layouts: 8.23 us -> 4.77 us
    all_gather x1, waiting for transfers between devices: 0.01 us -> 26.5 us  [body(): gathered = lax.all_gather(key_values, 'q', axis=0, tiled=True)]
    unnamed x1 -> x0, blocking collectives: 22.9 us -> none
    all_to_all x1, waiting for transfers between devices: 20.2 us -> 12.3 us  [body(): lax.all_to_all(outbox, ('p', 'y'), split_axis=0, concat_axis=0, tiled=True)]
    all_gather x1, blocking collectives: 39.6 us -> 37.4 us  [body(): plane_queries = lax.all_gather(queries, ('p', 'y'), axis=0, tiled=True)]
    unnamed x13 -> x10, local copies, waits for them, and re-layouts: 5.08 us -> 3.07 us
  transfers between devices with their start and end apart: 3 -> 3, of which waited for: 1 -> 2; matrix products, arithmetic and copies ran while one was open for 6% -> 4% of each run, Pallas kernels for 1% -> 1%
where the time goes in v1:
time: 141 us; the launch traced here: 139 us
  blocking collectives  53.6 us (38%)
  waiting for transfers between devices  38.9 us (28%)
  Pallas kernels  16.8 us (12%)
  between operations  15.5 us (11%)
  starting transfers between devices  6.21 us (4%)
  local copies, waits for them, and re-layouts  4.77 us (3%)
  other arithmetic  3.59 us (3%)
    all_gather x1, blocking collectives, body(): plane_queries = lax.all_gather(queries, ('p', 'y'), axis=0, tiled=True)  37.4 us
    all_gather x1, waiting for transfers between devices, body(): gathered = lax.all_gather(key_values, 'q', axis=0, tiled=True)  26.5 us
    all_gather x1, blocking collectives, body(): ours = lax.all_gather(stream_x, 'x', axis=0, tiled=True)  16.2 us
    all_to_all x1, waiting for transfers between devices, body(): lax.all_to_all(outbox, ('p', 'y'), split_axis=0, concat_axis=0, tiled=True)  12.3 us
    pallas_call x1, Pallas kernels, body(): pl.pallas_call(attention, in_specs=[SMEM, VMEM, VMEM, ANY], out_specs=VME...  10.5 us
    all_to_all x1, starting transfers between devices, body(): lax.all_to_all(outbox, ('p', 'y'), split_axis=0, concat_axis=0, tiled=True)  4.26 us
    unnamed x10, local copies, waits for them, and re-layouts  3.07 us
    pallas_call x1, Pallas kernels, body(): pl.pallas_call(combine, in_specs=[SMEM, ANY, ANY], out_specs=[VMEM, VMEM,...  2.89 us
  transfers between devices with their start and end apart: 3, of which 2 were waited for; matrix products, arithmetic and copies ran while one was open for 4% of the time, Pallas kernels for 1%

profile of v1, /device:TPU:6, one launch (start us, length us, event | category | flops | bytes accessed | tf_op | source)
XLA Modules:
  0.0 139.4 jit_solution(12935789957440236410)
XLA Ops:
  7.2 0.0 all-gather.2.cloned.1.call-start
  7.2 16.2 %all_gather.9.x_ref = bf16[1024,384]{1,0:T(8,128)(2,1)S(1)} all-gather(bf16[256,384]{1,0:T(8,128)(2,1)} %param.4), channel_id=1, replica_groups=mesh['q'=8,'p'=2,'y'=4,'x'=4,'c'=2] {'x'}, dimensions={0}, use_global_device_ids=true | all-gather | bytes 983040 | tf_op jit(solution)/shard_map/all_gather | solution.py:374
  23.4 1.9 %collective-permute-start = (bf16[1024,384]{1,0:T(8,128)(2,1)S(1)}, bf16[1024,384]{1,0:T(8,128)(2,1)S(1)}, u32[]{:S(2)}, u32[]{:S(2)}) collective-permute-start(bf16[1024,384]{1,0:T(8,128)(2,1)S(1)} %all_gather.9.x_ref), channel_id=1, source_target_pairs={{0,1},{1,0},{2,3},{3,2},{4,5},{5,4},{6,7},{7,6},{8,9},{9,8},{10,11... | collective-permute-start | bytes 2359304 | tf_op jit(solution)/shard_map/ppermute | solution.py:375
  25.3 0.7 select_reduce_fusion.3
  26.1 0.6 slice.10
  26.7 0.1 select_reduce_fusion.1
  26.8 0.0 copy-start
  26.8 2.0 %copy-done = bf16[3072,576]{0,1:T(8,128)(2,1)S(1)} copy-done((bf16[3072,576]{0,1:T(8,128)(2,1)S(1)}, bf16[3072,576]{0,1:T(8,128)(2,1)}, u32[]{:S(2)}) %copy-start) | copy-done | bytes 3538968
  28.8 0.0 copy-start.3
  28.8 0.0 copy-start.1
  28.8 1.0 shard_map.67.first_ref
  29.9 0.0 copy-done.3
  29.9 0.6 fusion.2.owner_ref
  30.5 0.5 fusion.1
  31.1 0.0 collective-permute-done.x_ref
  31.1 0.0 copy-done.1
  31.1 0.0 copy-start.4
  31.1 2.4 %shard_map.68 = (bf16[256,224]{1,0:T(8,128)(2,1)S(1)}, bf16[272,384]{1,0:T(8,128)(2,1)}) custom-call(s32[1]{0:T(128)S(6)} %sub.13.core_ref, bf16[1024,384]{1,0:T(8,128)(2,1)S(1)} %collective-permute-done.x_ref, bf16[576,3072]{1,0:T(8,128)(2,1)S(1)} %bitcast.13, f32[256,576]{1,0:T(8,128)S(1)} %shard_map.67.first_ref, ...), custom_call_target="tpu_custom_call" | custom-call | tf_op jit(solution)/shard_map/pallas_call | solution.py:402
  33.5 0.0 all-gather.2.cloned.1.call-update
  33.5 0.7 pad_add_fusion.info_ref
  34.2 0.1 iota_add_fusion
  34.2 0.0 copy-done.4
  34.2 0.1 select_reduce_fusion.2
  34.3 0.7 select_reduce_fusion.ends_ref
  35.1 37.4 %all_gather.11.q_ref = bf16[2048,224]{1,0:T(8,128)(2,1)} all-gather(bf16[256,224]{1,0:T(8,128)(2,1)S(1)} %get-tuple-element.17), channel_id=1, replica_groups=mesh['q'=8,'p'=2,'y'=4,'x'=4,'c'=2] {'p','y'}, dimensions={0}, use_global_device_ids=true | all-gather | bytes 1032192 | tf_op jit(solution)/shard_map/all_gather | solution.py:415
  72.5 26.5 %all-gather.2.cloned.1.call-done = bf16[2176,384]{1,0:T(8,128)(2,1)} async-done(((bf16[272,384]{1,0:T(8,128)(2,1)}), bf16[2176,384]{1,0:T(8,128)(2,1)}) %all-gather.2.cloned.1.call-update) | async-done | bytes 1671184 | tf_op jit(solution)/shard_map/all_gather | solution.py:413
  99.0 10.5 %shard_map.69 = bf16[8,208,384]{2,1,0:T(8,128)(2,1)} custom-call(s32[3]{0:T(128)} %pad_add_fusion.info_ref, bf16[2048,224]{1,0:T(8,128)(2,1)} %all_gather.11.q_ref, s32[8,256]{1,0:T(8,128)} %select_reduce_fusion.ends_ref, bf16[8,272,384]{2,1,0:T(8,128)(2,1)} %bitcast.15), custom_call_target="tpu_custom_call" | custom-call | tf_op jit(solution)/shard_map/pallas_call | solution.py:435
  109.5 4.3 %all-to-all-start = ((bf16[8,208,384]{2,1,0:T(8,128)(2,1)}), bf16[8,208,384]{2,1,0:T(8,128)(2,1)S(1)}, u32[]{:S(2)}, u32[]{:S(2)}) async-start(bf16[8,208,384]{2,1,0:T(8,128)(2,1)} %shard_map.69), calls=%async_computation | async-start | bytes 2555904 | tf_op jit(solution)/shard_map/all_to_all | solution.py:450
  113.8 0.5 slice.9
  114.3 0.6 slice.11
  116.2 12.3 %all-to-all-done.got_hbm = bf16[8,208,384]{2,1,0:T(8,128)(2,1)S(1)} async-done(((bf16[8,208,384]{2,1,0:T(8,128)(2,1)}), bf16[8,208,384]{2,1,0:T(8,128)(2,1)S(1)}, u32[]{:S(2)}, u32[]{:S(2)}) %all-to-all-start) | async-done | bytes 1277984 | tf_op jit(solution)/shard_map/all_to_all | solution.py:450
  128.5 0.0 copy-start.2
  128.5 1.1 copy-done.2
  129.6 2.9 %shard_map.70 = (bf16[192,256]{1,0:T(8,128)(2,1)}, f32[2,256]{1,0:T(2,128)}, bf16[8,8,8,384]{3,2,1,0:T(8,128)(2,1)}) custom-call(s32[1]{0:T(128)S(6)} %convert_element_type.30.flag_ref, bf16[8,26,8,384]{3,2,1,0:T(8,128)(2,1)} %bitcast.14, bf16[8,208,384]{2,1,0:T(8,128)(2,1)} %copy-done.2), custom_call_target="tpu_custom_call" | custom-call | tf_op jit(solution)/shard_map/pallas_call | solution.py:452
  (7 shorter events, 0.0 us)
Async XLA Ops:
  7.2 91.8 %all-gather.2.cloned.1.call-start = ((), (), s32[]{:S(2)}) async-start(), calls=%async_computation.1 | async-start | bytes 1880064 | tf_op jit(solution)/shard_map/all_gather | solution.py:413
  23.4 7.7 %collective-permute-start = (bf16[1024,384]{1,0:T(8,128)(2,1)S(1)}, bf16[1024,384]{1,0:T(8,128)(2,1)S(1)}, u32[]{:S(2)}, u32[]{:S(2)}) collective-permute-start(bf16[1024,384]{1,0:T(8,128)(2,1)S(1)} %all_gather.9.x_ref), channel_id=1, source_target_pairs={{0,1},{1,0},{2,3},{3,2},{4,5},{5,4},{6,7},{7,6},{8,9},{9,8},{10,11... | collective-permute-start | bytes 2359304 | tf_op jit(solution)/shard_map/ppermute | solution.py:375
  26.8 2.0 %copy-start = (bf16[3072,576]{0,1:T(8,128)(2,1)S(1)}, bf16[3072,576]{0,1:T(8,128)(2,1)}, u32[]{:S(2)}) copy-start(bf16[3072,576]{0,1:T(8,128)(2,1)} %param.5) | copy-start | bytes 10616836
  28.8 1.0 copy-start.3
  28.8 2.3 %copy-start.1 = (bf16[3072,576]{0,1:T(8,128)(2,1)S(1)}, bf16[3072,576]{0,1:T(8,128)(2,1)}, u32[]{:S(2)}) copy-start(bf16[3072,576]{0,1:T(8,128)(2,1)} %param.5) | copy-start | bytes 10616836
  31.1 3.2 %copy-start.4 = (s32[32]{0:T(128)S(1)}, s32[32]{0:T(128)}, u32[]{:S(2)}) copy-start(s32[32]{0:T(128)} %param.6) | copy-start | bytes 388
  109.5 19.0 %all-to-all-start = ((bf16[8,208,384]{2,1,0:T(8,128)(2,1)}), bf16[8,208,384]{2,1,0:T(8,128)(2,1)S(1)}, u32[]{:S(2)}, u32[]{:S(2)}) async-start(bf16[8,208,384]{2,1,0:T(8,128)(2,1)} %shard_map.69), calls=%async_computation | async-start | bytes 2555904 | tf_op jit(solution)/shard_map/all_to_all | solution.py:450
  128.5 1.1 copy-start.2
Sparse Core Ops, SparseCore 0:
  33.6 65.3 all-gather.1

commit v2 on v1

--- a/solution.py
+++ b/solution.py
@@ -64,7 +64,7 @@
 
 
 def rest_projection(
-    core_ref, x_ref, w_ref, first_ref, cos_ref, sin_ref, owner_ref, q_ref, kv_ref
+    core_ref, x_ref, w_ref, first_ref, cos_ref, sin_ref, owner_ref, q_ref, kva_ref, kvb_ref
 ):
     total = first_ref[...] + block_sum(core_ref[0], x_ref, w_ref)
     rows, columns = total.shape
@@ -87,17 +87,34 @@
         return jnp.where(lanes < HD, window(first), 0.0)
 
     key_values = pack_heads(rotated(96), plain(192), rotated(384), plain(480))
+    early = kva_ref.shape[0]
     for i in range(3):
-        kv_ref[:rows, 128 * i : 128 * i + 128] = key_values[i].astype(jnp.bfloat16)
-    extra = kv_ref.shape[0] - rows
-    kv_ref[rows:, :rows] = jnp.broadcast_to(owner_ref[...], (extra, rows)).astype(jnp.bfloat16)
-    kv_ref[rows:, rows:] = jnp.zeros((extra, 384 - rows), jnp.bfloat16)
+        part = key_values[i].astype(jnp.bfloat16)
+        kva_ref[:, 128 * i : 128 * i + 128] = part[:early]
+        kvb_ref[: rows - early, 128 * i : 128 * i + 128] = part[early:]
+    kvb_ref[rows - early :, :rows] = jnp.broadcast_to(owner_ref[...], (16, rows)).astype(
+        jnp.bfloat16
+    )
+    kvb_ref[rows - early :, rows:] = jnp.zeros((16, 384 - rows), jnp.bfloat16)
     q_ref[:, :128] = rotated(0).astype(jnp.bfloat16)
     q_ref[:, 128:] = rotated(288)[:, :HD].astype(jnp.bfloat16)
 
 
 def attention(
-    info_ref, q_ref, ends_ref, kv_hbm, out_ref, kv_ref, qs, scores, peaks, totals, contexts, kv_sems
+    info_ref,
+    own_ref,
+    other_ref,
+    ends_ref,
+    kva_hbm,
+    kvb_hbm,
+    out_ref,
+    kv_ref,
+    qs,
+    scores,
+    peaks,
+    totals,
+    contexts,
+    kv_sems,
 ):
     group, member, column = info_ref[0], info_ref[1], info_ref[2]
     groups = kv_ref.shape[0]
@@ -107,17 +124,28 @@
     page_rows = groups * CAP
     long_planes = 11 * groups * PAIR // 16
 
-    def fetch(k):
-        return pltpu.make_async_copy(kv_hbm.at[k], kv_ref.at[k], kv_sems.at[k])
+    early = kva_hbm.shape[1]
+
+    def fetches(k):
+        return (
+            pltpu.make_async_copy(
+                kva_hbm.at[k], kv_ref.at[k, pl.ds(0, early), :], kv_sems.at[k, 0]
+            ),
+            pltpu.make_async_copy(
+                kvb_hbm.at[k], kv_ref.at[k, pl.ds(early, kvb_hbm.shape[1]), :], kv_sems.at[k, 1]
+            ),
+        )
 
     least = jnp.where(group * PAIR < long_planes, 0, group - 1)
 
     def start_fetch(k, carry):
-        fetch(k).start()
+        for copy in fetches(k):
+            copy.start()
         return carry
 
     def wait_fetch(k, carry):
-        fetch(k).wait()
+        for copy in fetches(k):
+            copy.wait()
         return carry
 
     lax.fori_loop(least, group + 1, start_fetch, 0)
@@ -134,7 +162,7 @@
     ]
     lanes = lane_ids((chunk, 128))
 
-    def one_plane(h, waits):
+    def one_plane(h, q_ref, waits):
         plane = group * PAIR + h
         is_long = plane < long_planes
         low = jnp.where(is_long, 0, group - 1)
@@ -142,10 +170,7 @@
         count = group + 1 - low
 
         for first in range(0, rows, chunk):
-            start = h * rows + first
-            if not isinstance(start, int):
-                start = pl.multiple_of(start, chunk)
-            here = pl.ds(start, chunk)
+            here = slice(first, first + chunk)
             q1 = q_ref[here, 128 : 128 + HD].astype(jnp.float32)
             q1 = jnp.concatenate([q1, jnp.zeros((chunk, 128 - HD), jnp.float32)], axis=1)
             q1 = pltpu.roll(q1, 64, 1)
@@ -261,8 +286,8 @@
             out_ref[target, tail, :chunk] = jnp.transpose(spread, (1, 0))[:16].astype(jnp.bfloat16)
             out_ref[target, tail, chunk:] = jnp.zeros((16, 384 - chunk), jnp.bfloat16)
 
-    for h in range(PAIR):
-        one_plane(h, h == 0)
+    one_plane(member, own_ref, True)
+    one_plane(1 - member, other_ref, False)
 
     lax.fori_loop(0, least, wait_fetch, 0)
     lax.fori_loop(group + 1, groups, wait_fetch, 0)
@@ -289,25 +314,19 @@
             out_ref[t, 16 * two : 16 * two + 16, :] = total[16 * t : 16 * t + 16]
 
 
-def combine(
-    flag_ref, pages_hbm, got_hbm, att_ref, lse_ref, cache_ref, parts_ref, pages_ref, parts_sem, pages_sem
-):
-    count = parts_ref.shape[0]
+def combine(flag_ref, pages_ref, got_ref, att_ref, lse_ref, cache_ref):
+    count = got_ref.shape[0]
     groups = cache_ref.shape[0]
-    load = pltpu.make_async_copy(
-        got_hbm.at[:, pl.ds(groups * CAP, parts_ref.shape[1]), :], parts_ref, parts_sem
-    )
-    load.start()
-    load_pages = pltpu.make_async_copy(pages_hbm.at[:, pl.ds(0, groups)], pages_ref, pages_sem)
-    load_pages.start()
-    load.wait()
+    base = groups * CAP
+    for t in range(count):
+        cache_ref[:, t] = pages_ref[t, :groups]
     live = flag_ref[0] == 0
     mid = KEYS // 2
     shares = []
     for head in range(2):
         lses = []
         for i in range(count):
-            rows = parts_ref[i, mid : mid + 16, :KEYS].astype(jnp.float32)
+            rows = got_ref[i, base + mid : base + mid + 16, :KEYS].astype(jnp.float32)
             first = 3 * head
             lses.append(
                 rows[first : first + 1] + rows[first + 1 : first + 2] + rows[first + 2 : first + 3]
@@ -331,7 +350,8 @@
             jnp.where(lanes < 32, far0, far1),
         )
         for j in range(3):
-            part = parts_ref[i, :mid, 128 * j : 128 * j + 128].astype(jnp.float32) * spread[j]
+            part = got_ref[i, base : base + mid, 128 * j : 128 * j + 128]
+            part = part.astype(jnp.float32) * spread[j]
             sums[j] = part if sums[j] is None else sums[j] + part
     turned = [
         jnp.where(live, jnp.transpose(v, (1, 0)), 0.0).astype(jnp.bfloat16) for v in sums
@@ -340,9 +360,6 @@
     att_ref[128:, :mid] = turned[1][:64]
     att_ref[:64, mid:] = turned[1][64:]
     att_ref[64:, mid:] = turned[2]
-    load_pages.wait()
-    for t in range(count):
-        cache_ref[:, t] = pages_ref[t]
 
 
 SMEM = pl.BlockSpec(memory_space=pltpu.SMEM)
@@ -399,20 +416,26 @@
         out_shape=jax.ShapeDtypeStruct((tok_count, qkv_weight.shape[1]), jnp.float32),
         compiler_params=SMALL,
     )(core, in_vmem(ours), weight)
-    queries, key_values = pl.pallas_call(
+    early = 176
+    queries, keys_early, keys_late = pl.pallas_call(
         rest_projection,
         in_specs=[SMEM] + [VMEM] * 6,
-        out_specs=[VMEM, VMEM],
+        out_specs=[VMEM, VMEM, VMEM],
         out_shape=[
             jax.ShapeDtypeStruct((tok_count, 128 + HD), jnp.bfloat16),
-            jax.ShapeDtypeStruct((tok_count + 16, 384), jnp.bfloat16),
+            jax.ShapeDtypeStruct((early, 384), jnp.bfloat16),
+            jax.ShapeDtypeStruct((tok_count + 16 - early, 384), jnp.bfloat16),
         ],
         compiler_params=SMALL,
     )(1 - core, in_vmem(theirs), weight, in_vmem(half), in_vmem(cosine), in_vmem(sine), owner_row)
 
-    gathered = lax.all_gather(key_values, "q", axis=0, tiled=True)
-    queries, short_lengths = lax.optimization_barrier((queries, short_lengths))
-    plane_queries = lax.all_gather(queries, ("p", "y"), axis=0, tiled=True)
+    gathered = lax.all_gather(keys_early, "q", axis=0, tiled=True)
+    own_queries = lax.all_gather(queries, "y", axis=0, tiled=True)
+    other_queries = lax.ppermute(own_queries, "p", [(0, 1), (1, 0)])
+    own_queries, keys_late, short_lengths = lax.optimization_barrier(
+        (own_queries, keys_late, short_lengths)
+    )
+    gathered_late = lax.all_gather(keys_late, "q", axis=0, tiled=True)
 
     bounds = boundaries(short_lengths, plane_rows * long_planes)
     key_ids = (
@@ -424,8 +447,9 @@
     )
 
     info = jnp.stack([group, member, column]).astype(jnp.int32)
-    gathered, plane_queries, ends, info = lax.optimization_barrier(
-        (gathered, plane_queries, ends, info)
+    padding = (row_ids[:1] >= bounds[-1]).astype(jnp.int32)
+    gathered, gathered_late, own_queries, ends, info, padding = lax.optimization_barrier(
+        (gathered, gathered_late, own_queries, ends, info, padding)
     )
 
     most = max((long_planes - 1) // PAIR + 1, 2)
@@ -434,7 +458,7 @@
     box_rows = page_rows + tok_count // 2 + 16
     outbox = pl.pallas_call(
         attention,
-        in_specs=[SMEM, VMEM, VMEM, ANY],
+        in_specs=[SMEM, VMEM, VMEM, VMEM, ANY, ANY],
         out_specs=VMEM,
         out_shape=jax.ShapeDtypeStruct((targets, box_rows, 384), jnp.bfloat16),
         scratch_shapes=[
@@ -444,30 +468,31 @@
             pltpu.VMEM((2, plane_rows, 128), jnp.float32),
             pltpu.VMEM((2, plane_rows, 128), jnp.float32),
             pltpu.VMEM((2, plane_rows, 256), jnp.float32),
-            pltpu.SemaphoreType.DMA((groups,)),
+            pltpu.SemaphoreType.DMA((groups, 2)),
         ],
-    )(info, plane_queries, ends, gathered.reshape(groups, tok_count + 16, 384))
+    )(
+        info,
+        own_queries,
+        other_queries,
+        ends,
+        gathered.reshape(groups, early, 384),
+        gathered_late.reshape(groups, tok_count + 16 - early, 384),
+    )
     received = lax.all_to_all(outbox, ("p", "y"), split_axis=0, concat_axis=0, tiled=True)
-    padding = (row_ids[:1] >= bounds[-1]).astype(jnp.int32)
     attended, row_lse, kv_cache = pl.pallas_call(
         combine,
-        in_specs=[SMEM, ANY, ANY],
+        in_specs=[SMEM, VMEM, VMEM],
         out_specs=[VMEM, VMEM, VMEM],
         out_shape=[
             jax.ShapeDtypeStruct((2 * HD, tok_count), jnp.bfloat16),
             jax.ShapeDtypeStruct((2, tok_count), jnp.float32),
             jax.ShapeDtypeStruct((groups, targets, CAP, 384), jnp.bfloat16),
         ],
-        scratch_shapes=[
-            pltpu.VMEM((targets, tok_count // 2 + 16, 384), jnp.bfloat16),
-            pltpu.VMEM((targets, groups, CAP, 384), jnp.bfloat16),
-            pltpu.SemaphoreType.DMA,
-            pltpu.SemaphoreType.DMA,
-        ],
+        compiler_params=SMALL,
     )(
         padding,
-        received.reshape(targets, box_rows // CAP, CAP, 384),
-        received,
+        in_vmem(received.reshape(targets, box_rows // CAP, CAP, 384)),
+        in_vmem(received),
     )
     return (attended.T, row_lse, kv_cache.reshape(-1, 384))
 

time: 141 us -> 154 us (1.092)
  blocking collectives: 53.6 us -> 110 us
  waiting for transfers between devices: 38.9 us -> 0.02 us
  starting transfers between devices: 6.21 us -> 4.02 us
    all_gather x1 -> x2, blocking collectives: 37.4 us -> 77.1 us  [the longest x1 63.7 us: body(): gathered_late = lax.all_gather(keys_late, 'q', axis=0, tiled=True)]
    all_gather x1, waiting for transfers between devices: 26.5 us -> 0.01 us  [body(): gathered = lax.all_gather(keys_early, 'q', axis=0, tiled=True)]
    all_to_all x0 -> x1, blocking collectives: none -> 17 us  [body(): lax.all_to_all(outbox, ('p', 'y'), split_axis=0, concat_axis=0, tiled=True)]
    all_to_all x1 -> x0, waiting for transfers between devices: 12.3 us -> none  [body(): lax.all_to_all(outbox, ('p', 'y'), split_axis=0, concat_axis=0, tiled=True)]
    all_to_all x1 -> x0, starting transfers between devices: 4.26 us -> none  [body(): lax.all_to_all(outbox, ('p', 'y'), split_axis=0, concat_axis=0, tiled=True)]
    ppermute x0 -> x1, starting transfers between devices: none -> 2.07 us  [body(): other_queries = lax.ppermute(own_queries, 'p', [(0, 1), (1, 0)])]
  transfers between devices with their start and end apart: 3 -> 3, of which waited for: 2 -> 0; matrix products, arithmetic and copies ran while one was open for 4% -> 3% of each run, Pallas kernels for 1% -> 1%
where the time goes in v2:
time: 154 us; the launch traced here: 153 us
  blocking collectives  110 us (71%)
  Pallas kernels  15.6 us (10%)
  between operations  15.4 us (10%)
  local copies, waits for them, and re-layouts  4.46 us (3%)
  starting transfers between devices  4.02 us (3%)
  other arithmetic  3.59 us (2%)
    all_gather x1, blocking collectives, body(): gathered_late = lax.all_gather(keys_late, 'q', axis=0, tiled=True)  63.7 us
    all_to_all x1, blocking collectives, body(): lax.all_to_all(outbox, ('p', 'y'), split_axis=0, concat_axis=0, tiled=True)  17 us
    all_gather x1, blocking collectives, body(): ours = lax.all_gather(stream_x, 'x', axis=0, tiled=True)  16.2 us
    all_gather x1, blocking collectives, body(): own_queries = lax.all_gather(queries, 'y', axis=0, tiled=True)  13.3 us
    pallas_call x1, Pallas kernels, body(): pl.pallas_call(attention, in_specs=[SMEM, VMEM, VMEM, VMEM, ANY, ANY], ou...  10.6 us
  transfers between devices with their start and end apart: 3, of which 0 were waited for; matrix products, arithmetic and copies ran while one was open for 3% of the time, Pallas kernels for 1%

profile of v2, /device:TPU:6, one launch (start us, length us, event | category | flops | bytes accessed | tf_op | source)
XLA Modules:
  0.0 153.4 jit_solution(6527558726452246924)
XLA Ops:
  7.2 0.0 all-gather.2.cloned.1.call-start
  7.2 16.2 %all_gather.12.x_ref = bf16[1024,384]{1,0:T(8,128)(2,1)S(1)} all-gather(bf16[256,384]{1,0:T(8,128)(2,1)} %param.4), channel_id=1, replica_groups=mesh['q'=8,'p'=2,'y'=4,'x'=4,'c'=2] {'x'}, dimensions={0}, use_global_device_ids=true | all-gather | bytes 983040 | tf_op jit(solution)/shard_map/all_gather | solution.py:391
  23.4 1.9 %collective-permute-start = (bf16[1024,384]{1,0:T(8,128)(2,1)S(1)}, bf16[1024,384]{1,0:T(8,128)(2,1)S(1)}, u32[]{:S(2)}, u32[]{:S(2)}) collective-permute-start(bf16[1024,384]{1,0:T(8,128)(2,1)S(1)} %all_gather.12.x_ref), channel_id=1, source_target_pairs={{0,1},{1,0},{2,3},{3,2},{4,5},{5,4},{6,7},{7,6},{8,9},{9,8},{10,11... | collective-permute-start | bytes 2359304 | tf_op jit(solution)/shard_map/ppermute | solution.py:392
  25.3 0.7 select_reduce_fusion.3
  26.1 0.6 slice.9
  26.7 0.1 select_reduce_fusion.1
  26.8 0.0 copy-start
  26.8 2.0 %copy-done = bf16[3072,576]{0,1:T(8,128)(2,1)S(1)} copy-done((bf16[3072,576]{0,1:T(8,128)(2,1)S(1)}, bf16[3072,576]{0,1:T(8,128)(2,1)}, u32[]{:S(2)}) %copy-start) | copy-done | bytes 3538968
  28.8 0.0 copy-start.4
  28.8 0.0 copy-start.1
  28.8 1.0 shard_map.67.first_ref
  29.8 0.0 copy-done.4
  29.9 0.7 fusion.2.owner_ref
  30.5 0.5 fusion.1
  31.1 0.0 collective-permute-done.x_ref
  31.1 0.0 copy-done.1
  31.1 0.0 copy-start.5
  31.1 2.3 %shard_map.68 = (bf16[256,224]{1,0:T(8,128)(2,1)S(1)}, bf16[176,384]{1,0:T(8,128)(2,1)}, bf16[96,384]{1,0:T(8,128)(2,1)S(1)}) custom-call(s32[1]{0:T(128)S(6)} %sub.13.core_ref, bf16[1024,384]{1,0:T(8,128)(2,1)S(1)} %collective-permute-done.x_ref, bf16[576,3072]{1,0:T(8,128)(2,1)S(1)} %bitcast.14, f32[256,576]{1,0:T(8,128)S(1)} %shard_map.67.first_ref, ...), custom_call_target="tpu_custom_call" | custom-call | tf_op jit(solution)/shard_map/pallas_call | solution.py:420
  33.4 0.0 all-gather.2.cloned.1.call-update
  33.5 0.5 slice.10
  34.0 0.7 pad_add_fusion.info_ref
  34.6 0.1 iota_add_fusion
  34.7 13.3 %all_gather.14.own_ref = bf16[1024,224]{1,0:T(8,128)(2,1)S(1)} all-gather(bf16[256,224]{1,0:T(8,128)(2,1)S(1)} %get-tuple-element.19), channel_id=1, replica_groups=mesh['q'=8,'p'=2,'y'=4,'x'=4,'c'=2] {'y'}, dimensions={0}, use_global_device_ids=true | all-gather | bytes 573440 | tf_op jit(solution)/shard_map/all_gather | solution.py:433
  48.0 0.0 copy-start.2
  48.0 2.1 %collective-permute-start.1 = (bf16[1024,224]{1,0:T(8,128)(2,1)S(1)}, bf16[1024,224]{1,0:T(8,128)(2,1)S(1)}, u32[]{:S(2)}, u32[]{:S(2)}) collective-permute-start(bf16[1024,224]{1,0:T(8,128)(2,1)S(1)} %all_gather.14.own_ref), channel_id=1, source_target_pairs={{0,32},{32,0},{1,33},{33,1},{2,34},{34,2},{3,35},{35,3},{4,36},{36... | collective-permute-start | bytes 1376264 | tf_op jit(solution)/shard_map/ppermute | solution.py:434
  50.1 0.0 copy-done.5
  50.1 0.1 select_reduce_fusion.2
  50.2 0.6 slice.11
  52.0 0.7 select_reduce_fusion.ends_ref
  52.7 63.7 %all_gather.15 = bf16[768,384]{1,0:T(8,128)(2,1)} all-gather(bf16[96,384]{1,0:T(8,128)(2,1)S(1)} %get-tuple-element.21), channel_id=1, replica_groups=mesh['q'=8,'p'=2,'y'=4,'x'=4,'c'=2] {'q'}, dimensions={0}, use_global_device_ids=true | all-gather | bytes 663552 | tf_op jit(solution)/shard_map/all_gather | solution.py:438
  116.5 0.0 all-gather.2.cloned.1.call-done
  116.5 0.0 collective-permute-done.1.other_ref
  116.5 0.0 copy-start.3
  116.5 0.0 copy-done.2
  116.5 0.8 copy-done.3
  117.3 10.6 %shard_map.69 = bf16[8,208,384]{2,1,0:T(8,128)(2,1)} custom-call(s32[3]{0:T(128)} %pad_add_fusion.info_ref, bf16[1024,224]{1,0:T(8,128)(2,1)} %copy-done.2, bf16[1024,224]{1,0:T(8,128)(2,1)} %copy-done.3, s32[8,256]{1,0:T(8,128)} %select_reduce_fusion.ends_ref, bf16[8,176,384]{2,1,0:T(8,128)(2,1)} %bitcast.17, bf16[8,96,384]{2,1,0:T(8,128)(2,1)} %bitcast.16), custom_call_target="tpu_custom_call" | custom-call | tf_op jit(solution)/shard_map/pallas_call | solution.py:459
  127.9 17.0 %all_to_all.5.got_ref = bf16[8,208,384]{2,1,0:T(8,128)(2,1)S(1)} all-to-all(bf16[8,208,384]{2,1,0:T(8,128)(2,1)} %shard_map.69), channel_id=1, replica_groups=mesh['q'=8,'p'=2,'y'=4,'x'=4,'c'=2] {'p','y'}, dimensions={0} | all-to-all | bytes 2555904 | tf_op jit(solution)/shard_map/all_to_all | solution.py:481
  144.9 1.6 %shard_map.70 = (bf16[192,256]{1,0:T(8,128)(2,1)}, f32[2,256]{1,0:T(2,128)}, bf16[8,8,8,384]{3,2,1,0:T(8,128)(2,1)}) custom-call(s32[1]{0:T(128)S(6)} %convert_element_type.30.flag_ref, bf16[8,26,8,384]{3,2,1,0:T(8,128)(2,1)S(1)} %bitcast.15, bf16[8,208,384]{2,1,0:T(8,128)(2,1)S(1)} %all_to_all.5.got_ref), custom_call_target="tpu_custom_call" | custom-call | tf_op jit(solution)/shard_map/pallas_call | solution.py:482
  (7 shorter events, 0.0 us)
Async XLA Ops:
  7.2 109.3 %all-gather.2.cloned.1.call-start = ((), (), s32[]{:S(2)}) async-start(), calls=%async_computation.1 | async-start | bytes 1216512 | tf_op jit(solution)/shard_map/all_gather | solution.py:432
  23.4 7.7 %collective-permute-start = (bf16[1024,384]{1,0:T(8,128)(2,1)S(1)}, bf16[1024,384]{1,0:T(8,128)(2,1)S(1)}, u32[]{:S(2)}, u32[]{:S(2)}) collective-permute-start(bf16[1024,384]{1,0:T(8,128)(2,1)S(1)} %all_gather.12.x_ref), channel_id=1, source_target_pairs={{0,1},{1,0},{2,3},{3,2},{4,5},{5,4},{6,7},{7,6},{8,9},{9,8},{10,11... | collective-permute-start | bytes 2359304 | tf_op jit(solution)/shard_map/ppermute | solution.py:392
  26.8 2.0 %copy-start = (bf16[3072,576]{0,1:T(8,128)(2,1)S(1)}, bf16[3072,576]{0,1:T(8,128)(2,1)}, u32[]{:S(2)}) copy-start(bf16[3072,576]{0,1:T(8,128)(2,1)} %param.5) | copy-start | bytes 10616836
  28.8 1.0 copy-start.4
  28.8 2.3 %copy-start.1 = (bf16[3072,576]{0,1:T(8,128)(2,1)S(1)}, bf16[3072,576]{0,1:T(8,128)(2,1)}, u32[]{:S(2)}) copy-start(bf16[3072,576]{0,1:T(8,128)(2,1)} %param.5) | copy-start | bytes 10616836
  31.1 19.0 %copy-start.5 = (s32[32]{0:T(128)S(1)}, s32[32]{0:T(128)}, u32[]{:S(2)}) copy-start(s32[32]{0:T(128)} %param.6) | copy-start | bytes 388
  48.0 68.5 %copy-start.2 = (bf16[1024,224]{1,0:T(8,128)(2,1)}, bf16[1024,224]{1,0:T(8,128)(2,1)S(1)}, u32[]{:S(2)}) copy-start(bf16[1024,224]{1,0:T(8,128)(2,1)S(1)} %all_gather.14.own_ref) | copy-start | bytes 1376260
  48.0 68.4 %collective-permute-start.1 = (bf16[1024,224]{1,0:T(8,128)(2,1)S(1)}, bf16[1024,224]{1,0:T(8,128)(2,1)S(1)}, u32[]{:S(2)}, u32[]{:S(2)}) collective-permute-start(bf16[1024,224]{1,0:T(8,128)(2,1)S(1)} %all_gather.14.own_ref), channel_id=1, source_target_pairs={{0,32},{32,0},{1,33},{33,1},{2,34},{34,2},{3,35},{35,3},{4,36},{36... | collective-permute-start | bytes 1376264 | tf_op jit(solution)/shard_map/ppermute | solution.py:434
  116.5 0.8 copy-start.3
Sparse Core Ops, SparseCore 0:
  33.6 58.8 all-gather.1

commit v3 on v2

--- a/solution.py
+++ b/solution.py
@@ -64,7 +64,7 @@
 
 
 def rest_projection(
-    core_ref, x_ref, w_ref, first_ref, cos_ref, sin_ref, owner_ref, q_ref, kva_ref, kvb_ref
+    core_ref, x_ref, w_ref, first_ref, cos_ref, sin_ref, owner_ref, q_ref, kv_ref
 ):
     total = first_ref[...] + block_sum(core_ref[0], x_ref, w_ref)
     rows, columns = total.shape
@@ -87,15 +87,10 @@
         return jnp.where(lanes < HD, window(first), 0.0)
 
     key_values = pack_heads(rotated(96), plain(192), rotated(384), plain(480))
-    early = kva_ref.shape[0]
     for i in range(3):
-        part = key_values[i].astype(jnp.bfloat16)
-        kva_ref[:, 128 * i : 128 * i + 128] = part[:early]
-        kvb_ref[: rows - early, 128 * i : 128 * i + 128] = part[early:]
-    kvb_ref[rows - early :, :rows] = jnp.broadcast_to(owner_ref[...], (16, rows)).astype(
-        jnp.bfloat16
-    )
-    kvb_ref[rows - early :, rows:] = jnp.zeros((16, 384 - rows), jnp.bfloat16)
+        kv_ref[:rows, 128 * i : 128 * i + 128] = key_values[i].astype(jnp.bfloat16)
+    kv_ref[rows:, :rows] = jnp.broadcast_to(owner_ref[...], (16, rows)).astype(jnp.bfloat16)
+    kv_ref[rows:, rows:] = jnp.zeros((16, 384 - rows), jnp.bfloat16)
     q_ref[:, :128] = rotated(0).astype(jnp.bfloat16)
     q_ref[:, 128:] = rotated(288)[:, :HD].astype(jnp.bfloat16)
 
@@ -105,8 +100,7 @@
     own_ref,
     other_ref,
     ends_ref,
-    kva_hbm,
-    kvb_hbm,
+    kv_hbm,
     out_ref,
     kv_ref,
     qs,
@@ -124,28 +118,17 @@
     page_rows = groups * CAP
     long_planes = 11 * groups * PAIR // 16
 
-    early = kva_hbm.shape[1]
-
-    def fetches(k):
-        return (
-            pltpu.make_async_copy(
-                kva_hbm.at[k], kv_ref.at[k, pl.ds(0, early), :], kv_sems.at[k, 0]
-            ),
-            pltpu.make_async_copy(
-                kvb_hbm.at[k], kv_ref.at[k, pl.ds(early, kvb_hbm.shape[1]), :], kv_sems.at[k, 1]
-            ),
-        )
+    def fetch(k):
+        return pltpu.make_async_copy(kv_hbm.at[k], kv_ref.at[k], kv_sems.at[k])
 
     least = jnp.where(group * PAIR < long_planes, 0, group - 1)
 
     def start_fetch(k, carry):
-        for copy in fetches(k):
-            copy.start()
+        fetch(k).start()
         return carry
 
     def wait_fetch(k, carry):
-        for copy in fetches(k):
-            copy.wait()
+        fetch(k).wait()
         return carry
 
     lax.fori_loop(least, group + 1, start_fetch, 0)
@@ -416,26 +399,21 @@
         out_shape=jax.ShapeDtypeStruct((tok_count, qkv_weight.shape[1]), jnp.float32),
         compiler_params=SMALL,
     )(core, in_vmem(ours), weight)
-    early = 176
-    queries, keys_early, keys_late = pl.pallas_call(
+    queries, key_values = pl.pallas_call(
         rest_projection,
         in_specs=[SMEM] + [VMEM] * 6,
-        out_specs=[VMEM, VMEM, VMEM],
+        out_specs=[VMEM, VMEM],
         out_shape=[
             jax.ShapeDtypeStruct((tok_count, 128 + HD), jnp.bfloat16),
-            jax.ShapeDtypeStruct((early, 384), jnp.bfloat16),
-            jax.ShapeDtypeStruct((tok_count + 16 - early, 384), jnp.bfloat16),
+            jax.ShapeDtypeStruct((tok_count + 16, 384), jnp.bfloat16),
         ],
         compiler_params=SMALL,
     )(1 - core, in_vmem(theirs), weight, in_vmem(half), in_vmem(cosine), in_vmem(sine), owner_row)
 
-    gathered = lax.all_gather(keys_early, "q", axis=0, tiled=True)
+    gathered = lax.all_gather(key_values, "q", axis=0, tiled=True)
     own_queries = lax.all_gather(queries, "y", axis=0, tiled=True)
     other_queries = lax.ppermute(own_queries, "p", [(0, 1), (1, 0)])
-    own_queries, keys_late, short_lengths = lax.optimization_barrier(
-        (own_queries, keys_late, short_lengths)
-    )
-    gathered_late = lax.all_gather(keys_late, "q", axis=0, tiled=True)
+    own_queries, short_lengths = lax.optimization_barrier((own_queries, short_lengths))
 
     bounds = boundaries(short_lengths, plane_rows * long_planes)
     key_ids = (
@@ -448,8 +426,8 @@
 
     info = jnp.stack([group, member, column]).astype(jnp.int32)
     padding = (row_ids[:1] >= bounds[-1]).astype(jnp.int32)
-    gathered, gathered_late, own_queries, ends, info, padding = lax.optimization_barrier(
-        (gathered, gathered_late, own_queries, ends, info, padding)
+    gathered, own_queries, other_queries, ends, info, padding = lax.optimization_barrier(
+        (gathered, own_queries, other_queries, ends, info, padding)
     )
 
     most = max((long_planes - 1) // PAIR + 1, 2)
@@ -458,7 +436,7 @@
     box_rows = page_rows + tok_count // 2 + 16
     outbox = pl.pallas_call(
         attention,
-        in_specs=[SMEM, VMEM, VMEM, VMEM, ANY, ANY],
+        in_specs=[SMEM, VMEM, VMEM, VMEM, ANY],
         out_specs=VMEM,
         out_shape=jax.ShapeDtypeStruct((targets, box_rows, 384), jnp.bfloat16),
         scratch_shapes=[
@@ -468,15 +446,14 @@
             pltpu.VMEM((2, plane_rows, 128), jnp.float32),
             pltpu.VMEM((2, plane_rows, 128), jnp.float32),
             pltpu.VMEM((2, plane_rows, 256), jnp.float32),
-            pltpu.SemaphoreType.DMA((groups, 2)),
+            pltpu.SemaphoreType.DMA((groups,)),
         ],
     )(
         info,
         own_queries,
         other_queries,
         ends,
-        gathered.reshape(groups, early, 384),
-        gathered_late.reshape(groups, tok_count + 16 - early, 384),
+        gathered.reshape(groups, tok_count + 16, 384),
     )
     received = lax.all_to_all(outbox, ("p", "y"), split_axis=0, concat_axis=0, tiled=True)
     attended, row_lse, kv_cache = pl.pallas_call(

time: 154 us -> 142 us (0.922)
  blocking collectives: 110 us -> 49.1 us
  waiting for transfers between devices: 0.02 us -> 49.7 us
    all_gather x1 -> x0, blocking collectives: 63.7 us -> none  [body(): gathered_late = lax.all_gather(keys_late, 'q', axis=0, tiled=True)]
    all_gather x1, waiting for transfers between devices: 0.01 us -> 28.6 us  [body(): gathered = lax.all_gather(key_values, 'q', axis=0, tiled=True)]
    ppermute x1, waiting for transfers between devices: 0.01 us -> 21.1 us  [body(): other_queries = lax.ppermute(own_queries, 'p', [(0, 1), (1, 0)])]
    all_to_all x1, blocking collectives: 17 us -> 19.6 us  [body(): lax.all_to_all(outbox, ('p', 'y'), split_axis=0, concat_axis=0, tiled=True)]
  transfers between devices with their start and end apart: 3 -> 3, of which waited for: 0 -> 2; matrix products, arithmetic and copies ran while one was open for 3% -> 4% of each run, Pallas kernels for 1% -> 1%
where the time goes in v3:
time: 142 us; the launch traced here: 141 us
  waiting for transfers between devices  49.7 us (35%)
  blocking collectives  49.1 us (35%)
  Pallas kernels  15.5 us (11%)
  between operations  15.5 us (11%)
  starting transfers between devices  4.01 us (3%)
  local copies, waits for them, and re-layouts  3.73 us (3%)
  other arithmetic  3.59 us (3%)
    all_gather x1, waiting for transfers between devices, body(): gathered = lax.all_gather(key_values, 'q', axis=0, tiled=True)  28.6 us
    ppermute x1, waiting for transfers between devices, body(): other_queries = lax.ppermute(own_queries, 'p', [(0, 1), (1, 0)])  21.1 us
    all_to_all x1, blocking collectives, body(): lax.all_to_all(outbox, ('p', 'y'), split_axis=0, concat_axis=0, tiled=True)  19.6 us
    all_gather x1, blocking collectives, body(): ours = lax.all_gather(stream_x, 'x', axis=0, tiled=True)  16.2 us
    all_gather x1, blocking collectives, body(): own_queries = lax.all_gather(queries, 'y', axis=0, tiled=True)  13.3 us
    pallas_call x1, Pallas kernels, body(): pl.pallas_call(attention, in_specs=[SMEM, VMEM, VMEM, VMEM, ANY], out_spe...  10.5 us
  transfers between devices with their start and end apart: 3, of which 2 were waited for; matrix products, arithmetic and copies ran while one was open for 4% of the time, Pallas kernels for 1%

profile of v3, /device:TPU:6, one launch (start us, length us, event | category | flops | bytes accessed | tf_op | source)
XLA Modules:
  0.0 141.1 jit_solution(16684058811638502169)
XLA Ops:
  7.2 0.0 all-gather.2.cloned.1.call-start
  7.2 16.2 %all_gather.9.x_ref = bf16[1024,384]{1,0:T(8,128)(2,1)S(1)} all-gather(bf16[256,384]{1,0:T(8,128)(2,1)} %param.4), channel_id=1, replica_groups=mesh['q'=8,'p'=2,'y'=4,'x'=4,'c'=2] {'x'}, dimensions={0}, use_global_device_ids=true | all-gather | bytes 983040 | tf_op jit(solution)/shard_map/all_gather | solution.py:374
  23.4 1.9 %collective-permute-start = (bf16[1024,384]{1,0:T(8,128)(2,1)S(1)}, bf16[1024,384]{1,0:T(8,128)(2,1)S(1)}, u32[]{:S(2)}, u32[]{:S(2)}) collective-permute-start(bf16[1024,384]{1,0:T(8,128)(2,1)S(1)} %all_gather.9.x_ref), channel_id=1, source_target_pairs={{0,1},{1,0},{2,3},{3,2},{4,5},{5,4},{6,7},{7,6},{8,9},{9,8},{10,11... | collective-permute-start | bytes 2359304 | tf_op jit(solution)/shard_map/ppermute | solution.py:375
  25.3 0.7 select_reduce_fusion.3
  26.1 0.6 slice.9
  26.7 0.1 select_reduce_fusion.1
  26.8 0.0 copy-start
  26.8 2.0 %copy-done = bf16[3072,576]{0,1:T(8,128)(2,1)S(1)} copy-done((bf16[3072,576]{0,1:T(8,128)(2,1)S(1)}, bf16[3072,576]{0,1:T(8,128)(2,1)}, u32[]{:S(2)}) %copy-start) | copy-done | bytes 3538968
  28.8 0.0 copy-start.4
  28.8 0.0 copy-start.1
  28.8 1.0 shard_map.67.first_ref
  29.9 0.0 copy-done.4
  29.9 0.6 fusion.2.owner_ref
  30.5 0.5 fusion.1
  31.1 0.0 collective-permute-done.x_ref
  31.1 0.0 copy-done.1
  31.1 0.0 copy-start.5
  31.1 2.4 %shard_map.68 = (bf16[256,224]{1,0:T(8,128)(2,1)S(1)}, bf16[272,384]{1,0:T(8,128)(2,1)}) custom-call(s32[1]{0:T(128)S(6)} %sub.13.core_ref, bf16[1024,384]{1,0:T(8,128)(2,1)S(1)} %collective-permute-done.x_ref, bf16[576,3072]{1,0:T(8,128)(2,1)S(1)} %bitcast.13, f32[256,576]{1,0:T(8,128)S(1)} %shard_map.67.first_ref, ...), custom_call_target="tpu_custom_call" | custom-call | tf_op jit(solution)/shard_map/pallas_call | solution.py:402
  33.5 0.0 all-gather.2.cloned.1.call-update
  33.5 0.1 iota_add_fusion
  33.6 13.3 %all_gather.11.own_ref = bf16[1024,224]{1,0:T(8,128)(2,1)S(1)} all-gather(bf16[256,224]{1,0:T(8,128)(2,1)S(1)} %get-tuple-element.17), channel_id=1, replica_groups=mesh['q'=8,'p'=2,'y'=4,'x'=4,'c'=2] {'y'}, dimensions={0}, use_global_device_ids=true | all-gather | bytes 573440 | tf_op jit(solution)/shard_map/all_gather | solution.py:414
  46.9 0.0 copy-start.2
  46.9 2.1 %collective-permute-start.1 = (bf16[1024,224]{1,0:T(8,128)(2,1)S(1)}, bf16[1024,224]{1,0:T(8,128)(2,1)S(1)}, u32[]{:S(2)}, u32[]{:S(2)}) collective-permute-start(bf16[1024,224]{1,0:T(8,128)(2,1)S(1)} %all_gather.11.own_ref), channel_id=1, source_target_pairs={{0,32},{32,0},{1,33},{33,1},{2,34},{34,2},{3,35},{35,3},{4,36},{36... | collective-permute-start | bytes 1376264 | tf_op jit(solution)/shard_map/ppermute | solution.py:415
  49.0 0.7 pad_add_fusion.info_ref
  49.7 0.5 slice.10
  50.2 0.0 copy-done.5
  50.2 0.1 select_reduce_fusion.2
  50.3 0.6 slice.11
  52.2 0.7 select_reduce_fusion.ends_ref
  52.9 21.1 %collective-permute-done.1.other_ref = bf16[1024,224]{1,0:T(8,128)(2,1)S(1)} collective-permute-done((bf16[1024,224]{1,0:T(8,128)(2,1)S(1)}, bf16[1024,224]{1,0:T(8,128)(2,1)S(1)}, u32[]{:S(2)}, u32[]{:S(2)}) %collective-permute-start.1) | collective-permute-done | bytes 458784 | tf_op jit(solution)/shard_map/ppermute | solution.py:415
  74.0 0.0 copy-start.3
  74.0 28.6 %all-gather.2.cloned.1.call-done = bf16[2176,384]{1,0:T(8,128)(2,1)} async-done(((bf16[272,384]{1,0:T(8,128)(2,1)}), bf16[2176,384]{1,0:T(8,128)(2,1)}) %all-gather.2.cloned.1.call-update) | async-done | bytes 1671184 | tf_op jit(solution)/shard_map/all_gather | solution.py:413
  102.6 0.0 copy-done.2
  102.6 0.0 copy-done.3
  102.6 10.5 %shard_map.69 = bf16[8,208,384]{2,1,0:T(8,128)(2,1)} custom-call(s32[3]{0:T(128)} %pad_add_fusion.info_ref, bf16[1024,224]{1,0:T(8,128)(2,1)} %copy-done.2, bf16[1024,224]{1,0:T(8,128)(2,1)} %copy-done.3, s32[8,256]{1,0:T(8,128)} %select_reduce_fusion.ends_ref, bf16[8,272,384]{2,1,0:T(8,128)(2,1)} %bitcast.15), custom_call_target="tpu_custom_call" | custom-call | tf_op jit(solution)/shard_map/pallas_call | solution.py:437
  113.1 19.6 %all_to_all.5.got_ref = bf16[8,208,384]{2,1,0:T(8,128)(2,1)S(1)} all-to-all(bf16[8,208,384]{2,1,0:T(8,128)(2,1)} %shard_map.69), channel_id=1, replica_groups=mesh['q'=8,'p'=2,'y'=4,'x'=4,'c'=2] {'p','y'}, dimensions={0} | all-to-all | bytes 2555904 | tf_op jit(solution)/shard_map/all_to_all | solution.py:458
  132.6 1.6 %shard_map.70 = (bf16[192,256]{1,0:T(8,128)(2,1)}, f32[2,256]{1,0:T(2,128)}, bf16[8,8,8,384]{3,2,1,0:T(8,128)(2,1)}) custom-call(s32[1]{0:T(128)S(6)} %convert_element_type.30.flag_ref, bf16[8,26,8,384]{3,2,1,0:T(8,128)(2,1)S(1)} %bitcast.14, bf16[8,208,384]{2,1,0:T(8,128)(2,1)S(1)} %all_to_all.5.got_ref), custom_call_target="tpu_custom_call" | custom-call | tf_op jit(solution)/shard_map/pallas_call | solution.py:459
  (7 shorter events, 0.0 us)
Async XLA Ops:
  7.2 95.4 %all-gather.2.cloned.1.call-start = ((), (), s32[]{:S(2)}) async-start(), calls=%async_computation.1 | async-start | bytes 1880064 | tf_op jit(solution)/shard_map/all_gather | solution.py:413
  23.4 7.7 %collective-permute-start = (bf16[1024,384]{1,0:T(8,128)(2,1)S(1)}, bf16[1024,384]{1,0:T(8,128)(2,1)S(1)}, u32[]{:S(2)}, u32[]{:S(2)}) collective-permute-start(bf16[1024,384]{1,0:T(8,128)(2,1)S(1)} %all_gather.9.x_ref), channel_id=1, source_target_pairs={{0,1},{1,0},{2,3},{3,2},{4,5},{5,4},{6,7},{7,6},{8,9},{9,8},{10,11... | collective-permute-start | bytes 2359304 | tf_op jit(solution)/shard_map/ppermute | solution.py:375
  26.8 2.0 %copy-start = (bf16[3072,576]{0,1:T(8,128)(2,1)S(1)}, bf16[3072,576]{0,1:T(8,128)(2,1)}, u32[]{:S(2)}) copy-start(bf16[3072,576]{0,1:T(8,128)(2,1)} %param.5) | copy-start | bytes 10616836
  28.8 1.0 copy-start.4
  28.8 2.3 %copy-start.1 = (bf16[3072,576]{0,1:T(8,128)(2,1)S(1)}, bf16[3072,576]{0,1:T(8,128)(2,1)}, u32[]{:S(2)}) copy-start(bf16[3072,576]{0,1:T(8,128)(2,1)} %param.5) | copy-start | bytes 10616836
  31.1 19.1 %copy-start.5 = (s32[32]{0:T(128)S(1)}, s32[32]{0:T(128)}, u32[]{:S(2)}) copy-start(s32[32]{0:T(128)} %param.6) | copy-start | bytes 388
  46.9 55.6 %copy-start.2 = (bf16[1024,224]{1,0:T(8,128)(2,1)}, bf16[1024,224]{1,0:T(8,128)(2,1)S(1)}, u32[]{:S(2)}) copy-start(bf16[1024,224]{1,0:T(8,128)(2,1)S(1)} %all_gather.11.own_ref) | copy-start | bytes 1376260
  46.9 27.0 %collective-permute-start.1 = (bf16[1024,224]{1,0:T(8,128)(2,1)S(1)}, bf16[1024,224]{1,0:T(8,128)(2,1)S(1)}, u32[]{:S(2)}, u32[]{:S(2)}) collective-permute-start(bf16[1024,224]{1,0:T(8,128)(2,1)S(1)} %all_gather.11.own_ref), channel_id=1, source_target_pairs={{0,32},{32,0},{1,33},{33,1},{2,34},{34,2},{3,35},{35,3},{4,36},{36... | collective-permute-start | bytes 1376264 | tf_op jit(solution)/shard_map/ppermute | solution.py:415
  74.0 28.6 %copy-start.3 = (bf16[1024,224]{1,0:T(8,128)(2,1)}, bf16[1024,224]{1,0:T(8,128)(2,1)S(1)}, u32[]{:S(2)}) copy-start(bf16[1024,224]{1,0:T(8,128)(2,1)S(1)} %collective-permute-done.1.other_ref) | copy-start | bytes 1376260
Sparse Core Ops, SparseCore 0:
  33.6 68.8 all-gather.1

commit v4 on v3

--- a/solution.py
+++ b/solution.py
@@ -24,6 +24,7 @@
 
 PAIR = 2
 KEYS = 256
+SHORT_SUM = 4096
 MESH_Y = 4
 
 
@@ -150,7 +151,6 @@
         is_long = plane < long_planes
         low = jnp.where(is_long, 0, group - 1)
         masked_low = jnp.where(is_long, group, group - 1)
-        count = group + 1 - low
 
         for first in range(0, rows, chunk):
             here = slice(first, first + chunk)
@@ -162,14 +162,10 @@
             qs[span, 128:256] = jnp.where(lanes < 64, 0.0, q1).astype(jnp.bfloat16)
             qs[span, 256:] = jnp.where(lanes < 32, q1, 0.0).astype(jnp.bfloat16)
 
-        peaks[...] = jnp.full_like(peaks, neg_large)
-        totals[...] = jnp.zeros_like(totals)
-        contexts[...] = jnp.zeros_like(contexts)
-
         if waits:
             lax.fori_loop(least, group + 1, wait_fetch, 0)
 
-        def score(k, masked):
+        def score(k, masked, fresh=False):
             for head, span, first in parts:
                 s = lax.dot_general(
                     qs[span, key_cols[head]],
@@ -188,9 +184,10 @@
                     allowed = (key_ids <= row_ids) & (row_ids < ends_ref[pl.ds(k, 1), :])
                     s = jnp.where(allowed, s, neg_large)
                 scores[k - low, head, span, :] = s
-                peaks[head, span, :] = jnp.maximum(
-                    peaks[head, span, :], jnp.maximum(s[:, :128], s[:, 128:])
-                )
+                top = jnp.maximum(s[:, :128], s[:, 128:])
+                if not fresh:
+                    top = jnp.maximum(peaks[head, span, :], top)
+                peaks[head, span, :] = top
 
         def free_step(k, carry):
             score(k, False)
@@ -200,12 +197,9 @@
             score(k, True)
             return carry
 
+        score(group, True, True)
         lax.fori_loop(low, masked_low, free_step, 0)
-        lax.fori_loop(masked_low, group + 1, masked_step, 0)
-
-        @pl.when(count % 2 == 1)
-        def _():
-            scores[count] = jnp.full(scores.shape[1:], neg_large, jnp.float32)
+        lax.fori_loop(masked_low, group, masked_step, 0)
 
         tops = []
         for head, span, first in parts:
@@ -213,34 +207,34 @@
             tops.append(top)
             peaks[head, span, :] = jnp.broadcast_to(top * log2_scale, (chunk, 128))
 
-        def weigh(i, carry):
+        def weigh(k, fresh):
             for head, span, first in parts:
                 shift = peaks[head, span, :]
-                total = totals[head, span, :]
-                context = contexts[head, span, : value_width[head]]
-                for n in range(2):
-                    slot = 2 * i + n
-                    k = jnp.minimum(low + slot, group)
-                    s = scores[slot, head, span, :]
-                    left = jnp.exp2(s[:, :128] * log2_scale - shift)
-                    right = jnp.exp2(s[:, 128:] * log2_scale - shift)
-                    total = total + (left + right)
-                    p = jnp.concatenate(
-                        [left.astype(jnp.bfloat16), right.astype(jnp.bfloat16)], axis=1
-                    )
-                    context = context + jnp.dot(
-                        p, kv_ref[k, :KEYS, value_cols[head]], preferred_element_type=jnp.float32
-                    )
+                s = scores[k - low, head, span, :]
+                left = jnp.exp2(s[:, :128] * log2_scale - shift)
+                right = jnp.exp2(s[:, 128:] * log2_scale - shift)
+                total = left + right
+                p = jnp.concatenate([left.astype(jnp.bfloat16), right.astype(jnp.bfloat16)], axis=1)
+                context = jnp.dot(
+                    p, kv_ref[k, :KEYS, value_cols[head]], preferred_element_type=jnp.float32
+                )
+                if not fresh:
+                    total = totals[head, span, :] + total
+                    context = contexts[head, span, : value_width[head]] + context
                 totals[head, span, :] = total
                 contexts[head, span, : value_width[head]] = context
+
+        def weigh_step(k, carry):
+            weigh(k, False)
             return carry
 
-        lax.fori_loop(0, (count + 1) // 2, weigh, 0)
+        weigh(group, True)
+        lax.fori_loop(low, group, weigh_step, 0)
 
         for first in range(0, rows, chunk):
             span = slice(first, first + chunk)
             found = []
-            columns = []
+            spread = jnp.zeros((chunk, 128), jnp.float32)
             for head in range(2):
                 top = tops[head * (rows // chunk) + first // chunk]
                 denominator = jnp.sum(totals[head, span, :], axis=1, keepdims=True)
@@ -251,10 +245,19 @@
                 else:
                     context = pltpu.roll(contexts[head, span, :128], 96, 1)
                 found.append(jnp.where(lanes < HD, context / denominator, 0.0))
-                lse = top * score_scale + jnp.log(denominator)
+                spread = jnp.where(lanes == 2 * head, top, spread)
+                spread = jnp.where(lanes == 2 * head + 1, denominator, spread)
+            turned = jnp.transpose(spread, (1, 0))
+            pieces = []
+            for head in range(2):
+                lse = turned[2 * head : 2 * head + 1] * score_scale + jnp.log(
+                    turned[2 * head + 1 : 2 * head + 2]
+                )
                 coarse = lse.astype(jnp.bfloat16).astype(jnp.float32)
                 middle = (lse - coarse).astype(jnp.bfloat16).astype(jnp.float32)
-                columns += [coarse, middle, lse - coarse - middle]
+                pieces += [coarse, middle, lse - coarse - middle]
+            pieces.append(jnp.zeros((10, chunk), jnp.float32))
+            pieces = jnp.concatenate(pieces, axis=0).astype(jnp.bfloat16)
             target = h * MESH_Y + first // KEYS
             mid = chunk // 2
             packed = pack_heads(found[0][:mid], found[1][:mid], found[0][mid:], found[1][mid:])
@@ -262,11 +265,8 @@
                 out_ref[target, page_rows : page_rows + mid, 128 * i : 128 * i + 128] = packed[
                     i
                 ].astype(jnp.bfloat16)
-            spread = jnp.zeros((chunk, 128), jnp.float32)
-            for i, value in enumerate(columns):
-                spread = jnp.where(lanes == i, value, spread)
             tail = slice(page_rows + mid, page_rows + mid + 16)
-            out_ref[target, tail, :chunk] = jnp.transpose(spread, (1, 0))[:16].astype(jnp.bfloat16)
+            out_ref[target, tail, :chunk] = pieces
             out_ref[target, tail, chunk:] = jnp.zeros((16, 384 - chunk), jnp.bfloat16)
 
     one_plane(member, own_ref, True)
@@ -369,6 +369,7 @@
     plane_rows = tok_count * columns
     long_planes = groups * PAIR * 11 // 16
     bounds = boundaries(short_lengths, plane_rows * long_planes)
+    stream_end = plane_rows * long_planes + SHORT_SUM
 
     weight = in_vmem(qkv_weight.T)
     ours = lax.all_gather(stream_x, "x", axis=0, tiled=True)
@@ -389,7 +390,7 @@
     cosine = jnp.where(lane[None, :] < HD, jnp.cos(angle), 0.0)
     sine = jnp.sin(angle) * sign[None, :]
 
-    owner_row = jnp.where(row_ids < bounds[-1], cache_owner.reshape(tok_count), -1)
+    owner_row = jnp.where(row_ids < stream_end, cache_owner.reshape(tok_count), -1)
     owner_row = owner_row.astype(jnp.float32)[None, :]
 
     half = pl.pallas_call(
@@ -425,18 +426,18 @@
     )
 
     info = jnp.stack([group, member, column]).astype(jnp.int32)
-    padding = (row_ids[:1] >= bounds[-1]).astype(jnp.int32)
+    padding = (row_ids[:1] >= stream_end).astype(jnp.int32)
     gathered, own_queries, other_queries, ends, info, padding = lax.optimization_barrier(
         (gathered, own_queries, other_queries, ends, info, padding)
     )
 
     most = max((long_planes - 1) // PAIR + 1, 2)
-    slots = 2 * ((most + 1) // 2)
+    slots = most
     page_rows = groups * CAP
     box_rows = page_rows + tok_count // 2 + 16
     outbox = pl.pallas_call(
         attention,
-        in_specs=[SMEM, VMEM, VMEM, VMEM, ANY],
+        in_specs=[SMEM, VMEM, VMEM, VMEM, pl.BlockSpec(memory_space=pltpu.HBM)],
         out_specs=VMEM,
         out_shape=jax.ShapeDtypeStruct((targets, box_rows, 384), jnp.bfloat16),
         scratch_shapes=[
@@ -448,10 +449,11 @@
             pltpu.VMEM((2, plane_rows, 256), jnp.float32),
             pltpu.SemaphoreType.DMA((groups,)),
         ],
+        compiler_params=SMALL,
     )(
         info,
-        own_queries,
-        other_queries,
+        in_vmem(own_queries),
+        in_vmem(other_queries),
         ends,
         gathered.reshape(groups, tok_count + 16, 384),
     )

time: 142 us -> 140 us (0.986)
  waiting for transfers between devices: 49.7 us -> 52.3 us
  Pallas kernels: 15.5 us -> 13.5 us
  other arithmetic: 3.59 us -> 1.78 us
    ppermute x1, waiting for transfers between devices: 21.1 us -> 23.5 us  [body(): other_queries = lax.ppermute(own_queries, 'p', [(0, 1), (1, 0)])]
    pallas_call x1, Pallas kernels: 10.5 us -> 8.45 us  [body(): pl.pallas_call(attention, in_specs=[SMEM, VMEM, VMEM, VMEM, pl.BlockSpec(...]
    unnamed x12 -> x10, local copies, waits for them, and re-layouts: 2.02 us -> 3.75 us
  transfers between devices with their start and end apart: 3 -> 3, of which waited for: 2 -> 2; matrix products, arithmetic and copies ran while one was open for 4% -> 2% of each run, Pallas kernels for 1% -> 1%
where the time goes in v4:
time: 140 us; the launch traced here: 139 us
  waiting for transfers between devices  52.3 us (37%)
  blocking collectives  48.2 us (34%)
  between operations  14.8 us (11%)
  Pallas kernels  13.5 us (10%)
  local copies, waits for them, and re-layouts  4.26 us (3%)
  starting transfers between devices  4.01 us (3%)
  other arithmetic  1.78 us (1%)
    all_gather x1, waiting for transfers between devices, body(): gathered = lax.all_gather(key_values, 'q', axis=0, tiled=True)  28.8 us
    ppermute x1, waiting for transfers between devices, body(): other_queries = lax.ppermute(own_queries, 'p', [(0, 1), (1, 0)])  23.5 us
    all_to_all x1, blocking collectives, body(): lax.all_to_all(outbox, ('p', 'y'), split_axis=0, concat_axis=0, tiled=True)  18.7 us
    all_gather x1, blocking collectives, body(): ours = lax.all_gather(stream_x, 'x', axis=0, tiled=True)  16.2 us
    all_gather x1, blocking collectives, body(): own_queries = lax.all_gather(queries, 'y', axis=0, tiled=True)  13.4 us
    pallas_call x1, Pallas kernels, body(): pl.pallas_call(attention, in_specs=[SMEM, VMEM, VMEM, VMEM, pl.BlockSpec(...  8.45 us
    unnamed x10, local copies, waits for them, and re-layouts  3.75 us
  transfers between devices with their start and end apart: 3, of which 2 were waited for; matrix products, arithmetic and copies ran while one was open for 2% of the time, Pallas kernels for 1%

profile of v4, /device:TPU:6, one launch (start us, length us, event | category | flops | bytes accessed | tf_op | source)
XLA Modules:
  0.0 138.9 jit_solution(6704217220579354904)
XLA Ops:
  7.2 0.0 all-gather.2.cloned.1.call-start
  7.2 16.2 %all_gather.9.x_ref = bf16[1024,384]{1,0:T(8,128)(2,1)S(1)} all-gather(bf16[256,384]{1,0:T(8,128)(2,1)} %param.4), channel_id=1, replica_groups=mesh['q'=8,'p'=2,'y'=4,'x'=4,'c'=2] {'x'}, dimensions={0}, use_global_device_ids=true | all-gather | bytes 983040 | tf_op jit(solution)/shard_map/all_gather | solution.py:375
  23.4 1.9 %collective-permute-start = (bf16[1024,384]{1,0:T(8,128)(2,1)S(1)}, bf16[1024,384]{1,0:T(8,128)(2,1)S(1)}, u32[]{:S(2)}, u32[]{:S(2)}) collective-permute-start(bf16[1024,384]{1,0:T(8,128)(2,1)S(1)} %all_gather.9.x_ref), channel_id=1, source_target_pairs={{0,1},{1,0},{2,3},{3,2},{4,5},{5,4},{6,7},{7,6},{8,9},{9,8},{10,11... | collective-permute-start | bytes 2359304 | tf_op jit(solution)/shard_map/ppermute | solution.py:376
  25.3 0.7 select_reduce_fusion.3
  26.1 0.0 copy-start
  26.1 2.0 %copy-done = bf16[3072,576]{0,1:T(8,128)(2,1)S(1)} copy-done((bf16[3072,576]{0,1:T(8,128)(2,1)S(1)}, bf16[3072,576]{0,1:T(8,128)(2,1)}, u32[]{:S(2)}) %copy-start) | copy-done | bytes 3538968
  28.1 0.0 copy-start.3
  28.1 0.0 copy-start.1
  28.1 1.0 shard_map.67.first_ref
  29.1 0.1 select_reduce_fusion.1
  29.3 0.0 copy-done.3
  29.3 0.5 fusion.1
  29.8 0.0 collective-permute-done.x_ref
  29.8 0.3 copy-done.1
  30.1 0.0 copy-start.4
  30.1 2.4 %shard_map.68 = (bf16[256,224]{1,0:T(8,128)(2,1)S(1)}, bf16[272,384]{1,0:T(8,128)(2,1)}) custom-call(s32[1]{0:T(128)S(6)} %sub.13.core_ref, bf16[1024,384]{1,0:T(8,128)(2,1)S(1)} %collective-permute-done.x_ref, bf16[576,3072]{1,0:T(8,128)(2,1)S(1)} %bitcast.12, f32[256,576]{1,0:T(8,128)S(1)} %shard_map.67.first_ref, ...), custom_call_target="tpu_custom_call" | custom-call | tf_op jit(solution)/shard_map/pallas_call | solution.py:403
  32.5 0.0 all-gather.2.cloned.1.call-update
  32.6 0.1 iota_add_fusion
  32.6 13.4 %all_gather.11.own_ref = bf16[1024,224]{1,0:T(8,128)(2,1)S(1)} all-gather(bf16[256,224]{1,0:T(8,128)(2,1)S(1)} %get-tuple-element.17), channel_id=1, replica_groups=mesh['q'=8,'p'=2,'y'=4,'x'=4,'c'=2] {'y'}, dimensions={0}, use_global_device_ids=true | all-gather | bytes 573440 | tf_op jit(solution)/shard_map/all_gather | solution.py:415
  46.0 2.1 %collective-permute-start.1 = (bf16[1024,224]{1,0:T(8,128)(2,1)S(1)}, bf16[1024,224]{1,0:T(8,128)(2,1)S(1)}, u32[]{:S(2)}, u32[]{:S(2)}) collective-permute-start(bf16[1024,224]{1,0:T(8,128)(2,1)S(1)} %all_gather.11.own_ref), channel_id=1, source_target_pairs={{0,32},{32,0},{1,33},{33,1},{2,34},{34,2},{3,35},{35,3},{4,36},{36... | collective-permute-start | bytes 1376264 | tf_op jit(solution)/shard_map/ppermute | solution.py:416
  48.0 0.1 pad_add_fusion.info_ref
  48.1 0.5 slice.3
  49.3 0.0 copy-done.4
  49.3 0.1 select_reduce_fusion.2
  49.4 0.1 select_reduce_fusion.ends_ref
  49.5 23.5 %collective-permute-done.1.other_ref = bf16[1024,224]{1,0:T(8,128)(2,1)S(1)} collective-permute-done((bf16[1024,224]{1,0:T(8,128)(2,1)S(1)}, bf16[1024,224]{1,0:T(8,128)(2,1)S(1)}, u32[]{:S(2)}, u32[]{:S(2)}) %collective-permute-start.1) | collective-permute-done | bytes 458784 | tf_op jit(solution)/shard_map/ppermute | solution.py:416
  73.0 28.8 %all-gather.2.cloned.1.call-done = bf16[2176,384]{1,0:T(8,128)(2,1)} async-done(((bf16[272,384]{1,0:T(8,128)(2,1)}), bf16[2176,384]{1,0:T(8,128)(2,1)}) %all-gather.2.cloned.1.call-update) | async-done | bytes 1671184 | tf_op jit(solution)/shard_map/all_gather | solution.py:414
  101.8 0.0 copy-start.2
  101.8 1.4 %copy-done.2 = bf16[2176,384]{1,0:T(8,128)(2,1)S(1)} copy-done((bf16[2176,384]{1,0:T(8,128)(2,1)S(1)}, bf16[2176,384]{1,0:T(8,128)(2,1)}, u32[]{:S(2)}) %copy-start.2) | copy-done | bytes 1671192
  103.2 8.4 %shard_map.69 = bf16[8,208,384]{2,1,0:T(8,128)(2,1)S(1)} custom-call(s32[3]{0:T(128)S(1)} %pad_add_fusion.info_ref, bf16[1024,224]{1,0:T(8,128)(2,1)S(1)} %all_gather.11.own_ref, bf16[1024,224]{1,0:T(8,128)(2,1)S(1)} %collective-permute-done.1.other_ref, s32[8,256]{1,0:T(8,128)S(1)} %select_reduce_fusion.ends_ref, bf16[8,272,384]{2,1,0:T(8,128)(2,1)S(1)} %bitcast.14), custom_call_target="tpu_custom_call" | custom-call | tf_op jit(solution)/shard_map/pallas_call | solution.py:438
  111.7 18.7 %all_to_all.5.got_ref = bf16[8,208,384]{2,1,0:T(8,128)(2,1)S(1)} all-to-all(bf16[8,208,384]{2,1,0:T(8,128)(2,1)S(1)} %shard_map.69), channel_id=1, replica_groups=mesh['q'=8,'p'=2,'y'=4,'x'=4,'c'=2] {'p','y'}, dimensions={0} | all-to-all | bytes 2555904 | tf_op jit(solution)/shard_map/all_to_all | solution.py:460
  130.4 1.7 %shard_map.70 = (bf16[192,256]{1,0:T(8,128)(2,1)}, f32[2,256]{1,0:T(2,128)}, bf16[8,8,8,384]{3,2,1,0:T(8,128)(2,1)}) custom-call(s32[1]{0:T(128)S(6)} %convert_element_type.30.flag_ref, bf16[8,26,8,384]{3,2,1,0:T(8,128)(2,1)S(1)} %bitcast.13, bf16[8,208,384]{2,1,0:T(8,128)(2,1)S(1)} %all_to_all.5.got_ref), custom_call_target="tpu_custom_call" | custom-call | tf_op jit(solution)/shard_map/pallas_call | solution.py:461
  (8 shorter events, 0.1 us)
Async XLA Ops:
  7.2 94.6 %all-gather.2.cloned.1.call-start = ((), (), s32[]{:S(2)}) async-start(), calls=%async_computation.1 | async-start | bytes 1880064 | tf_op jit(solution)/shard_map/all_gather | solution.py:414
  23.4 6.4 %collective-permute-start = (bf16[1024,384]{1,0:T(8,128)(2,1)S(1)}, bf16[1024,384]{1,0:T(8,128)(2,1)S(1)}, u32[]{:S(2)}, u32[]{:S(2)}) collective-permute-start(bf16[1024,384]{1,0:T(8,128)(2,1)S(1)} %all_gather.9.x_ref), channel_id=1, source_target_pairs={{0,1},{1,0},{2,3},{3,2},{4,5},{5,4},{6,7},{7,6},{8,9},{9,8},{10,11... | collective-permute-start | bytes 2359304 | tf_op jit(solution)/shard_map/ppermute | solution.py:376
  26.1 2.0 %copy-start = (bf16[3072,576]{0,1:T(8,128)(2,1)S(1)}, bf16[3072,576]{0,1:T(8,128)(2,1)}, u32[]{:S(2)}) copy-start(bf16[3072,576]{0,1:T(8,128)(2,1)} %param.5) | copy-start | bytes 10616836
  28.1 1.1 copy-start.3
  28.1 2.0 %copy-start.1 = (bf16[3072,576]{0,1:T(8,128)(2,1)S(1)}, bf16[3072,576]{0,1:T(8,128)(2,1)}, u32[]{:S(2)}) copy-start(bf16[3072,576]{0,1:T(8,128)(2,1)} %param.5) | copy-start | bytes 10616836
  30.1 19.2 %copy-start.4 = (s32[32]{0:T(128)S(1)}, s32[32]{0:T(128)}, u32[]{:S(2)}) copy-start(s32[32]{0:T(128)} %param.6) | copy-start | bytes 388
  46.0 27.0 %collective-permute-start.1 = (bf16[1024,224]{1,0:T(8,128)(2,1)S(1)}, bf16[1024,224]{1,0:T(8,128)(2,1)S(1)}, u32[]{:S(2)}, u32[]{:S(2)}) collective-permute-start(bf16[1024,224]{1,0:T(8,128)(2,1)S(1)} %all_gather.11.own_ref), channel_id=1, source_target_pairs={{0,32},{32,0},{1,33},{33,1},{2,34},{34,2},{3,35},{35,3},{4,36},{36... | collective-permute-start | bytes 1376264 | tf_op jit(solution)/shard_map/ppermute | solution.py:416
  101.8 1.4 %copy-start.2 = (bf16[2176,384]{1,0:T(8,128)(2,1)S(1)}, bf16[2176,384]{1,0:T(8,128)(2,1)}, u32[]{:S(2)}) copy-start(bf16[2176,384]{1,0:T(8,128)(2,1)} %all-gather.2.cloned.1.call-done) | copy-start | bytes 5013508
Sparse Core Ops, SparseCore 0:
  32.7 69.0 all-gather.1

commit v5 on v4

--- a/solution.py
+++ b/solution.py
@@ -92,8 +92,12 @@
         kv_ref[:rows, 128 * i : 128 * i + 128] = key_values[i].astype(jnp.bfloat16)
     kv_ref[rows:, :rows] = jnp.broadcast_to(owner_ref[...], (16, rows)).astype(jnp.bfloat16)
     kv_ref[rows:, rows:] = jnp.zeros((16, 384 - rows), jnp.bfloat16)
-    q_ref[:, :128] = rotated(0).astype(jnp.bfloat16)
-    q_ref[:, 128:] = rotated(288)[:, :HD].astype(jnp.bfloat16)
+    q0 = rotated(0)
+    q1 = rotated(288)
+    mid = rows // 2
+    queries = pack_heads(q0[:mid], q1[:mid], q0[mid:], q1[mid:])
+    for i in range(3):
+        q_ref[:, 128 * i : 128 * i + 128] = queries[i].astype(jnp.bfloat16)
 
 
 def attention(
@@ -153,14 +157,19 @@
         masked_low = jnp.where(is_long, group, group - 1)
 
         for first in range(0, rows, chunk):
-            here = slice(first, first + chunk)
-            q1 = q_ref[here, 128 : 128 + HD].astype(jnp.float32)
-            q1 = jnp.concatenate([q1, jnp.zeros((chunk, 128 - HD), jnp.float32)], axis=1)
-            q1 = pltpu.roll(q1, 64, 1)
-            span = slice(first, first + chunk)
-            qs[span, :128] = q_ref[here, :128]
-            qs[span, 128:256] = jnp.where(lanes < 64, 0.0, q1).astype(jnp.bfloat16)
-            qs[span, 256:] = jnp.where(lanes < 32, q1, 0.0).astype(jnp.bfloat16)
+            mid = chunk // 2
+            short_lanes = lane_ids((mid, 128))
+            block = q_ref[first // 2 : first // 2 + mid, :].astype(jnp.float32)
+            for side in range(2):
+                begin = 2 * HD * side
+                q0 = pltpu.roll(block, (384 - begin) % 384, 1)[:, :128]
+                q1 = pltpu.roll(block, (384 - begin - HD + 64) % 384, 1)[:, :256]
+                span = slice(first + side * mid, first + side * mid + mid)
+                qs[span, :128] = jnp.where(short_lanes < HD, q0, 0.0).astype(jnp.bfloat16)
+                qs[span, 128:256] = jnp.where(short_lanes < 64, 0.0, q1[:, :128]).astype(
+                    jnp.bfloat16
+                )
+                qs[span, 256:] = jnp.where(short_lanes < 32, q1[:, 128:], 0.0).astype(jnp.bfloat16)
 
         if waits:
             lax.fori_loop(least, group + 1, wait_fetch, 0)
@@ -405,7 +414,7 @@
         in_specs=[SMEM] + [VMEM] * 6,
         out_specs=[VMEM, VMEM],
         out_shape=[
-            jax.ShapeDtypeStruct((tok_count, 128 + HD), jnp.bfloat16),
+            jax.ShapeDtypeStruct((tok_count // 2, 384), jnp.bfloat16),
             jax.ShapeDtypeStruct((tok_count + 16, 384), jnp.bfloat16),
         ],
         compiler_params=SMALL,
@@ -449,7 +458,6 @@
             pltpu.VMEM((2, plane_rows, 256), jnp.float32),
             pltpu.SemaphoreType.DMA((groups,)),
         ],
-        compiler_params=SMALL,
     )(
         info,
         in_vmem(own_queries),

time: 140 us -> 139 us (level)
  waiting for transfers between devices: 52.3 us -> 49.7 us
    ppermute x1, waiting for transfers between devices: 23.5 us -> 19.5 us  [body(): other_queries = lax.ppermute(own_queries, 'p', [(0, 1), (1, 0)])]
    all_to_all x1, blocking collectives: 18.7 us -> 20.6 us  [body(): lax.all_to_all(outbox, ('p', 'y'), split_axis=0, concat_axis=0, tiled=True)]
    unnamed x10 -> x8, local copies, waits for them, and re-layouts: 3.75 us -> 2.31 us
where the time goes in v5:
time: 139 us; the launch traced here: 138 us
  waiting for transfers between devices  49.7 us (36%)
  blocking collectives  49.4 us (36%)
  between operations  14.9 us (11%)
  Pallas kernels  13.6 us (10%)
  starting transfers between devices  4.32 us (3%)
  local copies, waits for them, and re-layouts  2.88 us (2%)
  other arithmetic  2.86 us (2%)
    all_gather x1, waiting for transfers between devices, body(): gathered = lax.all_gather(key_values, 'q', axis=0, tiled=True)  30.2 us
    all_to_all x1, blocking collectives, body(): lax.all_to_all(outbox, ('p', 'y'), split_axis=0, concat_axis=0, tiled=True)  20.6 us
    ppermute x1, waiting for transfers between devices, body(): other_queries = lax.ppermute(own_queries, 'p', [(0, 1), (1, 0)])  19.5 us
    all_gather x1, blocking collectives, body(): ours = lax.all_gather(stream_x, 'x', axis=0, tiled=True)  16.2 us
    all_gather x1, blocking collectives, body(): own_queries = lax.all_gather(queries, 'y', axis=0, tiled=True)  12.6 us
    pallas_call x1, Pallas kernels, body(): pl.pallas_call(attention, in_specs=[SMEM, VMEM, VMEM, VMEM, pl.BlockSpec(...  8.58 us
  transfers between devices with their start and end apart: 3, of which 2 were waited for; matrix products, arithmetic and copies ran while one was open for 2% of the time, Pallas kernels for 1%

profile of v5, /device:TPU:6, one launch (start us, length us, event | category | flops | bytes accessed | tf_op | source)
XLA Modules:
  0.0 137.6 jit_solution(3831122628575675460)
XLA Ops:
  7.2 0.0 all-gather.2.cloned.1.call-start
  7.2 16.2 %all_gather.9.x_ref = bf16[1024,384]{1,0:T(8,128)(2,1)S(1)} all-gather(bf16[256,384]{1,0:T(8,128)(2,1)} %param.4), channel_id=1, replica_groups=mesh['q'=8,'p'=2,'y'=4,'x'=4,'c'=2] {'x'}, dimensions={0}, use_global_device_ids=true | all-gather | bytes 983040 | tf_op jit(solution)/shard_map/all_gather | solution.py:384
  23.4 1.9 %collective-permute-start = (bf16[1024,384]{1,0:T(8,128)(2,1)S(1)}, bf16[1024,384]{1,0:T(8,128)(2,1)S(1)}, u32[]{:S(2)}, u32[]{:S(2)}) collective-permute-start(bf16[1024,384]{1,0:T(8,128)(2,1)S(1)} %all_gather.9.x_ref), channel_id=1, source_target_pairs={{0,1},{1,0},{2,3},{3,2},{4,5},{5,4},{6,7},{7,6},{8,9},{9,8},{10,11... | collective-permute-start | bytes 2359304 | tf_op jit(solution)/shard_map/ppermute | solution.py:385
  25.3 0.7 select_reduce_fusion.3
  26.1 0.0 copy-start
  26.1 2.0 %copy-done = bf16[3072,576]{0,1:T(8,128)(2,1)S(1)} copy-done((bf16[3072,576]{0,1:T(8,128)(2,1)S(1)}, bf16[3072,576]{0,1:T(8,128)(2,1)}, u32[]{:S(2)}) %copy-start) | copy-done | bytes 3538968
  28.1 0.0 copy-start.2
  28.1 0.0 copy-start.1
  28.1 1.0 shard_map.67.first_ref
  29.1 0.1 select_reduce_fusion.1
  29.3 0.0 copy-done.2
  29.3 0.5 fusion.1
  29.8 0.0 collective-permute-done.x_ref
  29.8 0.3 copy-done.1
  30.1 0.0 copy-start.3
  30.1 2.4 %shard_map.68 = (bf16[128,384]{1,0:T(8,128)(2,1)S(1)}, bf16[272,384]{1,0:T(8,128)(2,1)}) custom-call(s32[1]{0:T(128)S(6)} %sub.13.core_ref, bf16[1024,384]{1,0:T(8,128)(2,1)S(1)} %collective-permute-done.x_ref, bf16[576,3072]{1,0:T(8,128)(2,1)S(1)} %bitcast.12, f32[256,576]{1,0:T(8,128)S(1)} %shard_map.67.first_ref, ...), custom_call_target="tpu_custom_call" | custom-call | tf_op jit(solution)/shard_map/pallas_call | solution.py:412
  32.5 0.0 all-gather.2.cloned.1.call-update
  32.6 0.6 slice.3
  33.8 0.6 pad_add_fusion.info_ref
  34.4 0.1 iota_add_fusion
  34.5 12.6 %all_gather.11.own_ref = bf16[512,384]{1,0:T(8,128)(2,1)S(1)} all-gather(bf16[128,384]{1,0:T(8,128)(2,1)S(1)} %get-tuple-element.17), channel_id=1, replica_groups=mesh['q'=8,'p'=2,'y'=4,'x'=4,'c'=2] {'y'}, dimensions={0}, use_global_device_ids=true | all-gather | bytes 491520 | tf_op jit(solution)/shard_map/all_gather | solution.py:424
  47.1 2.4 %collective-permute-start.1 = (bf16[512,384]{1,0:T(8,128)(2,1)S(1)}, bf16[512,384]{1,0:T(8,128)(2,1)S(1)}, u32[]{:S(2)}, u32[]{:S(2)}) collective-permute-start(bf16[512,384]{1,0:T(8,128)(2,1)S(1)} %all_gather.11.own_ref), channel_id=1, source_target_pairs={{0,32},{32,0},{1,33},{33,1},{2,34},{34,2},{3,35},{35,3},{4,36},{36... | collective-permute-start | bytes 1179656 | tf_op jit(solution)/shard_map/ppermute | solution.py:425
  49.4 0.0 copy-done.3
  49.5 0.1 select_reduce_fusion.2
  49.6 0.7 select_reduce_fusion.ends_ref
  50.3 19.5 %collective-permute-done.1.other_ref = bf16[512,384]{1,0:T(8,128)(2,1)S(1)} collective-permute-done((bf16[512,384]{1,0:T(8,128)(2,1)S(1)}, bf16[512,384]{1,0:T(8,128)(2,1)S(1)}, u32[]{:S(2)}, u32[]{:S(2)}) %collective-permute-start.1) | collective-permute-done | bytes 393248 | tf_op jit(solution)/shard_map/ppermute | solution.py:425
  69.8 30.2 %all-gather.2.cloned.1.call-done = bf16[2176,384]{1,0:T(8,128)(2,1)} async-done(((bf16[272,384]{1,0:T(8,128)(2,1)}), bf16[2176,384]{1,0:T(8,128)(2,1)}) %all-gather.2.cloned.1.call-update) | async-done | bytes 1671184 | tf_op jit(solution)/shard_map/all_gather | solution.py:423
  99.9 8.6 %shard_map.69 = bf16[8,208,384]{2,1,0:T(8,128)(2,1)} custom-call(s32[3]{0:T(128)} %pad_add_fusion.info_ref, bf16[512,384]{1,0:T(8,128)(2,1)S(1)} %all_gather.11.own_ref, bf16[512,384]{1,0:T(8,128)(2,1)S(1)} %collective-permute-done.1.other_ref, s32[8,256]{1,0:T(8,128)} %select_reduce_fusion.ends_ref, bf16[8,272,384]{2,1,0:T(8,128)(2,1)} %bitcast.14), custom_call_target="tpu_custom_call" | custom-call | tf_op jit(solution)/shard_map/pallas_call | solution.py:447
  108.5 20.6 %all_to_all.5.got_ref = bf16[8,208,384]{2,1,0:T(8,128)(2,1)S(1)} all-to-all(bf16[8,208,384]{2,1,0:T(8,128)(2,1)} %shard_map.69), channel_id=1, replica_groups=mesh['q'=8,'p'=2,'y'=4,'x'=4,'c'=2] {'p','y'}, dimensions={0} | all-to-all | bytes 2555904 | tf_op jit(solution)/shard_map/all_to_all | solution.py:468
  129.1 1.6 %shard_map.70 = (bf16[192,256]{1,0:T(8,128)(2,1)}, f32[2,256]{1,0:T(2,128)}, bf16[8,8,8,384]{3,2,1,0:T(8,128)(2,1)}) custom-call(s32[1]{0:T(128)S(6)} %convert_element_type.30.flag_ref, bf16[8,26,8,384]{3,2,1,0:T(8,128)(2,1)S(1)} %bitcast.13, bf16[8,208,384]{2,1,0:T(8,128)(2,1)S(1)} %all_to_all.5.got_ref), custom_call_target="tpu_custom_call" | custom-call | tf_op jit(solution)/shard_map/pallas_call | solution.py:469
  (8 shorter events, 0.1 us)
Async XLA Ops:
  7.2 92.8 %all-gather.2.cloned.1.call-start = ((), (), s32[]{:S(2)}) async-start(), calls=%async_computation.1 | async-start | bytes 1880064 | tf_op jit(solution)/shard_map/all_gather | solution.py:423
  23.4 6.4 %collective-permute-start = (bf16[1024,384]{1,0:T(8,128)(2,1)S(1)}, bf16[1024,384]{1,0:T(8,128)(2,1)S(1)}, u32[]{:S(2)}, u32[]{:S(2)}) collective-permute-start(bf16[1024,384]{1,0:T(8,128)(2,1)S(1)} %all_gather.9.x_ref), channel_id=1, source_target_pairs={{0,1},{1,0},{2,3},{3,2},{4,5},{5,4},{6,7},{7,6},{8,9},{9,8},{10,11... | collective-permute-start | bytes 2359304 | tf_op jit(solution)/shard_map/ppermute | solution.py:385
  26.1 2.0 %copy-start = (bf16[3072,576]{0,1:T(8,128)(2,1)S(1)}, bf16[3072,576]{0,1:T(8,128)(2,1)}, u32[]{:S(2)}) copy-start(bf16[3072,576]{0,1:T(8,128)(2,1)} %param.5) | copy-start | bytes 10616836
  28.1 1.1 copy-start.2
  28.1 2.0 %copy-start.1 = (bf16[3072,576]{0,1:T(8,128)(2,1)S(1)}, bf16[3072,576]{0,1:T(8,128)(2,1)}, u32[]{:S(2)}) copy-start(bf16[3072,576]{0,1:T(8,128)(2,1)} %param.5) | copy-start | bytes 10616836
  30.1 19.3 %copy-start.3 = (s32[32]{0:T(128)S(1)}, s32[32]{0:T(128)}, u32[]{:S(2)}) copy-start(s32[32]{0:T(128)} %param.6) | copy-start | bytes 388
  47.1 22.7 %collective-permute-start.1 = (bf16[512,384]{1,0:T(8,128)(2,1)S(1)}, bf16[512,384]{1,0:T(8,128)(2,1)S(1)}, u32[]{:S(2)}, u32[]{:S(2)}) collective-permute-start(bf16[512,384]{1,0:T(8,128)(2,1)S(1)} %all_gather.11.own_ref), channel_id=1, source_target_pairs={{0,32},{32,0},{1,33},{33,1},{2,34},{34,2},{3,35},{35,3},{4,36},{36... | collective-permute-start | bytes 1179656 | tf_op jit(solution)/shard_map/ppermute | solution.py:425
Sparse Core Ops, SparseCore 0:
  32.7 67.2 all-gather.1
